TPU v7x, 512 devices: a whole 4x8x8 slice. The times are simulated.
512 devices in a mesh: ctx: 32 (over z, x_hi, core), ch: 16 (over y, x_lo).
Axes of the slice: x: 4 (x_hi: 2, x_lo: 2; x = x_hi * 2 + x_lo), y: 8, z: 8, core: 2. Of those that a mesh axis runs over, the one named last changes fastest.
Arguments:
- output_gate: bfloat16 [16384, 4096], P('ctx', 'ch'), may hold values from -6 to 6
- input_gate: bfloat16 [16384, 4096], P('ctx', 'ch'), may hold values from -6 to 6
- value_input: bfloat16 [16384, 4096], P('ctx', 'ch'), may hold values from -6 to 6
- short_filter: float32 [128, 4096], P(None, 'ch'), may hold values from -0.5 to 0.5
- long_filter: float32 [16384, 256], P('ctx', 'ch'), may hold values from -0.046875 to 0.046875
- skip_gain: float32 [4096], P('ch'), may hold values from -4 to 4
Outputs:
- mixed: bfloat16 [16384, 4096], P('ctx', 'ch')
All inputs are finite; a program needn't handle non-finite values.
Results may differ from a plain program's by a relative error of at most 0.001.
Values may be sent and summed in bfloat16 or wider, within the bound.
A program may use at most 64 MiB of HBM per device.

v0:
```python
import math

import jax
import jax.numpy as jnp
from jax import lax
from jax.sharding import PartitionSpec as P

HIGHEST = lax.Precision.HIGHEST


def passed_along(block, axis, distance):
    devices = range(lax.axis_size(axis))
    route = [(i - distance, i) for i in devices if i - distance in devices]
    return lax.ppermute(block, axis, route)


def depthwise(extended, filter_taps):
    kernel = filter_taps[::-1][:, None, :]
    result = lax.conv_general_dilated(
        extended[None],
        kernel,
        (1,),
        "VALID",
        dimension_numbers=("NWC", "WIO", "NWC"),
        feature_group_count=extended.shape[1],
        precision=HIGHEST,
    )
    return result[0]


def rotate(real_part, imag_part, cosine, sine):
    return (real_part * cosine - imag_part * sine, real_part * sine + imag_part * cosine)


def table_apply(pattern, cosine, sine, real_part, imag_part):
    out_real = jnp.einsum(pattern, cosine, real_part, precision=HIGHEST) - jnp.einsum(
        pattern, sine, imag_part, precision=HIGHEST
    )
    out_imag = jnp.einsum(pattern, cosine, imag_part, precision=HIGHEST) + jnp.einsum(
        pattern, sine, real_part, precision=HIGHEST
    )
    return (out_real, out_imag)


def dft_table(length, sign):
    index_vals = jnp.arange(length, dtype=jnp.int32)
    exponent = index_vals[:, None] * index_vals[None, :] % length
    angle = sign * 2.0 * math.pi * exponent.astype(jnp.float32) / length
    return (jnp.cos(angle), jnp.sin(angle))


def channel_local(signal, filt):
    length, cols = signal.shape
    fft_length = 2 * length
    size_a = math.gcd(length, 1 << fft_length.bit_length() // 2)
    size_b = fft_length // size_a
    half_b = size_b // 2
    pair_cols = cols // 2
    paired = signal.reshape(half_b, size_a, pair_cols, 2)
    sig_real = paired[..., 0]
    sig_imag = paired[..., 1]
    filt_real = filt.reshape(half_b, size_a, pair_cols, 2)[..., 0]
    b_cos, b_sin = dft_table(size_b, -1.0)
    in_cos = b_cos[:, :half_b]
    in_sin = b_sin[:, :half_b]
    data_real, data_imag = table_apply("kb,bap->kap", in_cos, in_sin, sig_real, sig_imag)
    spec_real = jnp.einsum("kb,bap->kap", in_cos, filt_real, precision=HIGHEST)
    spec_imag = jnp.einsum("kb,bap->kap", in_sin, filt_real, precision=HIGHEST)
    fine_index = jnp.arange(size_b, dtype=jnp.int32)
    coarse_index = jnp.arange(size_a, dtype=jnp.int32)
    exponent = fine_index[:, None] * coarse_index[None, :] % fft_length
    tw_angle = -2.0 * math.pi * exponent.astype(jnp.float32) / fft_length
    tw_cos = jnp.cos(tw_angle)[:, :, None]
    tw_sin = jnp.sin(tw_angle)[:, :, None]
    data_real, data_imag = rotate(data_real, data_imag, tw_cos, tw_sin)
    spec_real, spec_imag = rotate(spec_real, spec_imag, tw_cos, tw_sin)
    a_cos, a_sin = dft_table(size_a, -1.0)
    data_real, data_imag = table_apply("ka,bap->bkp", a_cos, a_sin, data_real, data_imag)
    spec_real, spec_imag = table_apply("ka,bap->bkp", a_cos, a_sin, spec_real, spec_imag)
    prod_real = data_real * spec_real - data_imag * spec_imag
    prod_imag = data_real * spec_imag + data_imag * spec_real
    back_real, back_imag = table_apply("ak,bkp->bap", a_cos, -a_sin, prod_real, prod_imag)
    back_real, back_imag = rotate(back_real, back_imag, tw_cos, -tw_sin)
    final_real, final_imag = table_apply(
        "bk,kap->bap", b_cos[:half_b], -b_sin[:half_b], back_real, back_imag
    )
    joined = jnp.stack([final_real, final_imag], axis=-1).reshape(length, cols)
    return joined / fft_length


def local(output_gate, input_gate, value_input, short_filter, long_filter, skip_gain):
    row_count, chan_count = value_input.shape
    group_total = long_filter.shape[1]
    tap_count = short_filter.shape[0]
    earlier = passed_along(value_input[row_count - tap_count + 1 :], "ctx", 1)
    extended = jnp.concatenate([earlier, value_input], axis=0).astype(jnp.float32)
    gated = input_gate.astype(jnp.float32) * depthwise(extended, short_filter)
    widened = jnp.repeat(long_filter, chan_count // group_total, axis=1)
    moved = (
        lax.all_to_all(gated, "ctx", split_axis=1, concat_axis=0, tiled=True),
        lax.all_to_all(widened, "ctx", split_axis=1, concat_axis=0, tiled=True),
    )
    convolved = channel_local(moved[0], moved[1])
    long_out = lax.all_to_all(convolved, "ctx", split_axis=0, concat_axis=1, tiled=True)
    mixed = output_gate.astype(jnp.float32) * (long_out + skip_gain[None, :] * gated)
    return mixed.astype(jnp.bfloat16)


def solution(mesh):
    placed = (
        P("ctx", "ch"),
        P("ctx", "ch"),
        P("ctx", "ch"),
        P(None, "ch"),
        P("ctx", "ch"),
        P("ch"),
    )
    return jax.shard_map(
        local, mesh=mesh, in_specs=placed, out_specs=P("ctx", "ch"), check_vma=False
    )
```

profile of v0, /device:TPU:1, one launch (start us, length us, event | category | flops | bytes accessed | tf_op | source)
XLA Modules:
  0.0 104.1 jit_solution(16083406796192630755)
XLA Ops:
  0.0 0.9 slice.38
  0.9 6.0 %collective-permute-start = (bf16[127,256]{1,0:T(8,128)(2,1)S(1)}, bf16[127,256]{1,0:T(8,128)(2,1)S(1)}, u32[]{:S(2)}, u32[]{:S(2)}) collective-permute-start(bf16[127,256]{1,0:T(8,128)(2,1)S(1)} %slice.38), channel_id=1, source_target_pairs={{0,16},{16,32},{32,48},{48,64},{64,80},{80,96},{96,112},{112,128},... | collective-permute-start | bytes 195080 | tf_op jit(solution)/shard_map/ppermute | solution.py:14
  7.0 0.9 broadcast_in_dim.26
  7.9 11.4 %all-to-all-start.1 = ((f32[512,32,8]{0,2,1:T(8,128)}), f32[512,32,8]{0,2,1:T(8,128)S(1)}, u32[]{:S(2)}, u32[]{:S(2)}) async-start(f32[512,32,8]{0,2,1:T(8,128)} %broadcast_in_dim.26), calls=%async_computation.1 | async-start | bytes 1048576 | tf_op jit(solution)/shard_map/all_to_all | solution.py:101
  21.1 11.6 %fusion.2 = f32[1,512,256]{2,0,1:T(1,128)S(1)} fusion(bf16[1,639,256]{2,1,0:T(8,128)(2,1)S(1)} %maximum_bitcast_fusion, f32[128,1,256]{2,0,1:T(8,128)S(1)} %bitcast.117), kind=kOutput, calls=%fused_computation.12 | convolution fusion | flops 201326592 | bytes 982528 | tf_op jit(solution)/shard_map/conv_general_dilated | solution.py:19
  32.8 1.0 copy.44
  33.8 2.3 %all-to-all-done.1 = f32[512,32,8]{0,2,1:T(8,128)S(1)} async-done(((f32[512,32,8]{0,2,1:T(8,128)}), f32[512,32,8]{0,2,1:T(8,128)S(1)}, u32[]{:S(2)}, u32[]{:S(2)}) %all-to-all-start.1) | async-done | bytes 524320 | tf_op jit(solution)/shard_map/all_to_all | solution.py:101
  36.2 7.6 %all-to-all-start = ((f32[512,32,8]{0,2,1:T(8,128)}), f32[512,32,8]{0,2,1:T(8,128)S(1)}, u32[]{:S(2)}, u32[]{:S(2)}) async-start(f32[512,32,8]{0,2,1:T(8,128)} %bitcast.4), calls=%async_computation | async-start | bytes 1048576 | tf_op jit(solution)/shard_map/all_to_all | solution.py:100
  44.2 0.6 fusion.40
  44.8 0.6 fusion.41
  45.4 1.6 %fusion.27 = f32[128,4,256]{2,0,1:T(8,128)S(1)} fusion(f32[128,256,4]{1,0,2:T(8,128)S(1)} %fusion.40, f32[128,256,4]{1,0,2:T(8,128)S(1)} %fusion.41, f32[128,256]{1,0:T(8,128)S(1)} %get-tuple-element.7, f32[128,256]{1,0:T(8,128)S(1)} %get-tuple-element.8), kind=kOutput, calls=%fused_computation.55 | convolution fusion | flops 403963904 | bytes 1835008 | tf_op jit(solution)/shard_map/ka,bap->bkp/dot_general | solution.py:39
  46.9 1.6 %fusion.31 = f32[128,4,256]{2,0,1:T(8,128)S(1)} fusion(f32[128,256,4]{1,0,2:T(8,128)S(1)} %fusion.40, f32[128,256,4]{1,0,2:T(8,128)S(1)} %fusion.41, f32[128,256]{1,0:T(8,128)S(1)} %get-tuple-element.7, f32[128,256]{1,0:T(8,128)S(1)} %get-tuple-element.8), kind=kOutput, calls=%fused_computation.59 | convolution fusion | flops 403963904 | bytes 1835008 | tf_op jit(solution)/shard_map/ka,bap->bkp/dot_general | solution.py:36
  48.5 1.6 %convolution_add_fusion.2 = f32[128,4,256]{2,0,1:T(8,128)S(1)} fusion(f32[128,4,256]{2,0,1:T(8,128)S(1)} %fusion.27, f32[128,256,4]{1,0,2:T(8,128)S(1)} %fusion.40, f32[128,256,4]{1,0,2:T(8,128)S(1)} %fusion.41, f32[128,256]{1,0:T(8,128)S(1)} %get-tuple-element.7, f32[128,256]{1,0:T(8,128)S(1)} %get-tuple-element.8), kind=kOutput, calls=%fused_computation.4 | convolution fusion | flops 404094976 | bytes 2359296 | tf_op jit(solution)/shard_map/ka,bap->bkp/dot_general | solution.py:39
  50.1 1.6 %convolution_subtract_fusion.2 = f32[128,4,256]{2,0,1:T(8,128)S(1)} fusion(f32[128,4,256]{2,0,1:T(8,128)S(1)} %fusion.31, f32[128,256,4]{1,0,2:T(8,128)S(1)} %fusion.40, f32[128,256,4]{1,0,2:T(8,128)S(1)} %fusion.41, f32[128,256]{1,0:T(8,128)S(1)} %get-tuple-element.7, f32[128,256]{1,0:T(8,128)S(1)} %get-tuple-element.8), kind=kOutput, calls=%fused_computation.6 | convolution fusion | flops 404094976 | bytes 2359296 | tf_op jit(solution)/shard_map/ka,bap->bkp/dot_general | solution.py:36
  51.7 8.8 %all-to-all-done = f32[512,32,8]{0,2,1:T(8,128)S(1)} async-done(((f32[512,32,8]{0,2,1:T(8,128)}), f32[512,32,8]{0,2,1:T(8,128)S(1)}, u32[]{:S(2)}, u32[]{:S(2)}) %all-to-all-start) | async-done | bytes 524320 | tf_op jit(solution)/shard_map/all_to_all | solution.py:100
  60.9 0.7 copy-done.3
  61.6 0.6 fusion.39
  62.2 0.6 fusion.38
  63.0 0.6 convolution_add_fusion
  63.6 0.6 convolution_subtract_fusion
  64.2 1.8 %fusion.29 = f32[128,4,256]{2,0,1:T(8,128)S(1)} fusion(f32[128,256,4]{1,0,2:T(8,128)S(1)} %convolution_add_fusion, f32[128,256,4]{1,0,2:T(8,128)S(1)} %convolution_subtract_fusion, f32[128,256]{1,0:T(8,128)S(1)} %get-tuple-element.7, f32[128,256]{1,0:T(8,128)S(1)} %get-tuple-element.8), kind=kOutput, calls=%fused_computation.57 | convolution fusion | flops 403963904 | bytes 1835008 | tf_op jit(solution)/shard_map/ka,bap->bkp/dot_general | solution.py:39
  66.0 1.6 %fusion.33 = f32[128,4,256]{2,0,1:T(8,128)S(1)} fusion(f32[128,256,4]{1,0,2:T(8,128)S(1)} %convolution_add_fusion, f32[128,256,4]{1,0,2:T(8,128)S(1)} %convolution_subtract_fusion, f32[128,256]{1,0:T(8,128)S(1)} %get-tuple-element.7, f32[128,256]{1,0:T(8,128)S(1)} %get-tuple-element.8), kind=kOutput, calls=%fused_computation.61 | convolution fusion | flops 403963904 | bytes 1835008 | tf_op jit(solution)/shard_map/ka,bap->bkp/dot_general | solution.py:36
  67.5 1.6 %convolution_subtract_fusion.3 = f32[128,4,256]{2,0,1:T(8,128)S(1)} fusion(f32[128,4,256]{2,0,1:T(8,128)S(1)} %fusion.33, f32[128,256,4]{1,0,2:T(8,128)S(1)} %convolution_add_fusion, f32[128,256,4]{1,0,2:T(8,128)S(1)} %convolution_subtract_fusion, f32[128,256]{1,0:T(8,128)S(1)} %get-tuple-element.7, f32[128,256]{1,0:T(8,128)S(1)} %get-tuple-element.8), kind=kOutput, calls=%fused_computation.7 | convolution fusion | flops 404094976 | bytes 2359296 | tf_op jit(solution)/shard_map/ka,bap->bkp/dot_general | solution.py:36
  69.1 1.6 %multiply_subtract_fusion.1 = (f32[128,4,256]{2,0,1:T(8,128)S(1)}, f32[128,4,256]{2,0,1:T(8,128)S(1)}) fusion(f32[128,4,256]{2,0,1:T(8,128)S(1)} %convolution_add_fusion.2, f32[128,4,256]{2,0,1:T(8,128)S(1)} %convolution_subtract_fusion.3, f32[128,4,256]{2,0,1:T(8,128)S(1)} %convolution_subtract_fusion.2, f32[128,4,256]{2,0,1:T(8,128)S(1)} %fusion.29, ...), kind=kOutput, calls=%fused_computation.32 | convolution fusion | flops 404881408 | bytes 4456448 | tf_op jit(solution)/shard_map/ka,bap->bkp/dot_general | solution.py:39
  70.8 1.6 %fusion.14 = f32[128,4,256]{2,0,1:T(8,128)S(1)} fusion(f32[128,4,256]{2,0,1:T(8,128)S(1)} %get-tuple-element.5), kind=kOutput, calls=%fused_computation.26 | convolution fusion | flops 403570688 | bytes 1048576 | tf_op jit(solution)/shard_map/ak,bkp->bap/dot_general | solution.py:36
  72.3 1.6 %fusion.10 = f32[128,4,256]{2,0,1:T(8,128)S(1)} fusion(f32[128,4,256]{2,0,1:T(8,128)S(1)} %get-tuple-element.6), kind=kOutput, calls=%fused_computation.22 | convolution fusion | flops 403570688 | bytes 1048576 | tf_op jit(solution)/shard_map/ak,bkp->bap/dot_general | solution.py:39
  73.9 1.6 %convolution_subtract_fusion.1 = f32[128,4,256]{2,0,1:T(8,128)S(1)} fusion(f32[128,4,256]{2,0,1:T(8,128)S(1)} %fusion.14, f32[128,4,256]{2,0,1:T(8,128)S(1)} %get-tuple-element.6), kind=kOutput, calls=%fused_computation.3 | convolution fusion | flops 403767296 | bytes 1572864 | tf_op jit(solution)/shard_map/ak,bkp->bap/dot_general | solution.py:36
  75.5 1.6 %convolution_add_fusion.1 = f32[128,4,256]{2,0,1:T(8,128)S(1)} fusion(f32[128,4,256]{2,0,1:T(8,128)S(1)} %fusion.10, f32[128,4,256]{2,0,1:T(8,128)S(1)} %get-tuple-element.5), kind=kOutput, calls=%fused_computation.2 | convolution fusion | flops 403767296 | bytes 1572864 | tf_op jit(solution)/shard_map/ak,bkp->bap/dot_general | solution.py:39
  77.1 0.7 fusion.4
  79.9 22.5 %all_to_all.45 = f32[32,512,8]{1,2,0:T(8,128)S(1)} all-to-all(f32[32,512,8]{1,2,0:T(8,128)S(1)} %copy.57), channel_id=1, replica_groups=mesh['ctx'=32,'ch'=16] {'ctx'}, dimensions={0} | all-to-all | bytes 1048576 | tf_op jit(solution)/shard_map/all_to_all | solution.py:104
  102.6 0.7 copy-done.6
  103.3 0.8 multiply_convert_fusion
  (40 shorter events, 5.2 us)
Async XLA Ops:
  0.0 6.9 %copy-start.8 = (f32[512,16]{0,1:T(8,128)S(1)}, f32[512,16]{0,1:T(8,128)}, u32[]{:S(2)}) copy-start(f32[512,16]{0,1:T(8,128)} %param.10) | copy-start | bytes 98308
  0.9 20.1 %collective-permute-start = (bf16[127,256]{1,0:T(8,128)(2,1)S(1)}, bf16[127,256]{1,0:T(8,128)(2,1)S(1)}, u32[]{:S(2)}, u32[]{:S(2)}) collective-permute-start(bf16[127,256]{1,0:T(8,128)(2,1)S(1)} %slice.38), channel_id=1, source_target_pairs={{0,16},{16,32},{32,48},{48,64},{64,80},{80,96},{96,112},{112,128},... | collective-permute-start | bytes 195080 | tf_op jit(solution)/shard_map/ppermute | solution.py:14
  7.9 28.3 %all-to-all-start.1 = ((f32[512,32,8]{0,2,1:T(8,128)}), f32[512,32,8]{0,2,1:T(8,128)S(1)}, u32[]{:S(2)}, u32[]{:S(2)}) async-start(f32[512,32,8]{0,2,1:T(8,128)} %broadcast_in_dim.26), calls=%async_computation.1 | async-start | bytes 1048576 | tf_op jit(solution)/shard_map/all_to_all | solution.py:101
  19.6 25.2 %copy-start.2 = (f32[128,128]{1,0:T(8,128)}, f32[128,128]{1,0:T(8,128)S(1)}, u32[]{:S(2)}) copy-start(f32[128,128]{1,0:T(8,128)S(1)} %fusion.76) | copy-start | bytes 196612
  19.6 1.1 %copy-start.7 = (f32[128,256]{1,0:T(8,128)S(1)}, f32[128,256]{1,0:T(8,128)}, u32[]{:S(2)}) copy-start(f32[128,256]{1,0:T(8,128)} %param.9) | copy-start | bytes 393220
  20.1 1.0 copy-start.4
  21.0 23.2 %copy-start = (f32[128,128]{1,0:T(8,128)}, f32[128,128]{1,0:T(8,128)S(1)}, u32[]{:S(2)}) copy-start(f32[128,128]{1,0:T(8,128)S(1)} %fusion.75) | copy-start | bytes 196612
  21.1 11.6 %copy-start.5 = (bf16[512,256]{1,0:T(8,128)(2,1)S(1)}, bf16[512,256]{1,0:T(8,128)(2,1)}, u32[]{:S(2)}) copy-start(bf16[512,256]{1,0:T(8,128)(2,1)} %param.7) | copy-start | bytes 786436
  36.2 24.3 %all-to-all-start = ((f32[512,32,8]{0,2,1:T(8,128)}), f32[512,32,8]{0,2,1:T(8,128)S(1)}, u32[]{:S(2)}, u32[]{:S(2)}) async-start(f32[512,32,8]{0,2,1:T(8,128)} %bitcast.4), calls=%async_computation | async-start | bytes 1048576 | tf_op jit(solution)/shard_map/all_to_all | solution.py:100
  60.8 0.8 copy-start.3
  62.2 0.8 copy-start.1
  102.4 1.0 copy-start.6
  102.4 1.0 copy-start.9
where the time goes:
time: 105 us; the launch traced here: 104 us
  matrix products  36.3 us (35%)
  starting transfers between devices  25.1 us (24%)
  blocking collectives  22.5 us (21%)
  waiting for transfers between devices  11.1 us (11%)
  local copies, waits for them, and re-layouts  6.17 us (6%)
  other arithmetic  2.53 us (2%)
    all_to_all x1, blocking collectives, local(): lax.all_to_all(convolved, 'ctx', split_axis=0, concat_axis=1, tiled=True)  22.5 us
    conv_general_dilated x1, matrix products, depthwise(): lax.conv_general_dilated(extended[None], kernel, (1,), 'VALID', dimension...  11.6 us
    all_to_all x1, starting transfers between devices, local(): lax.all_to_all(widened, 'ctx', split_axis=1, concat_axis=0, tiled=True)  11.4 us
    all_to_all x1, waiting for transfers between devices, local(): lax.all_to_all(gated, 'ctx', split_axis=1, concat_axis=0, tiled=True)  8.76 us
    all_to_all x1, starting transfers between devices, local(): lax.all_to_all(gated, 'ctx', split_axis=1, concat_axis=0, tiled=True)  7.63 us
    dot_general x5, matrix products, table_apply(): jnp.einsum(pattern, cosine, imag_part, precision=HIGHEST)  6.23 us
    ppermute x1, starting transfers between devices, passed_along(): return lax.ppermute(block, axis, route)  6.03 us
    dot_general x5, matrix products, table_apply(): jnp.einsum(pattern, sine, real_part, precision=HIGHEST)  5.84 us
  transfers between devices with their start and end apart: 3, of which 2 were waited for; matrix products, arithmetic and copies ran while one was open for 22% of the time, Pallas kernels for 0%

commit v1 on v0

v1 whole, which is shorter than its diff:
```python
import functools
import math

import jax
import jax.numpy as jnp
import numpy as np
from jax import lax
from jax.experimental import pallas as pl
from jax.experimental.pallas import tpu as pltpu
from jax.sharding import PartitionSpec as P

LANES = 128
OWN = 8
HALF = 4
F32 = jnp.float32
BF16 = jnp.bfloat16


def split_np(table):
    high = table.astype(BF16)
    low = (table - high.astype(np.float32)).astype(BF16)
    return high, low


def tables(rows):
    length = rows * LANES
    n1 = np.arange(rows)
    n2 = np.arange(LANES)
    first = np.pi * n1[None, :] * LANES / (2 * length) - 2 * np.pi * ((n1[:, None] * n1[None, :]) % rows) / rows
    twist = np.pi * n2[None, :] / (2 * length) - 2 * np.pi * ((n1[:, None] * n2[None, :]) % length) / length
    second = -2 * np.pi * ((n2[:, None] * n2[None, :]) % LANES) / LANES
    col = np.concatenate([np.cos(first), np.sin(first)], 0).astype(np.float32)
    col_hi, col_lo = split_np(col)
    col_fwd = np.concatenate([col_hi, col_hi, col_lo], 1)
    back = np.concatenate([np.cos(first).T, np.sin(first).T], 1).astype(np.float32)
    back_hi, back_lo = split_np(back)
    col_inv = np.concatenate([back_hi, back_lo], 0)
    cos2, sin2 = np.cos(second), np.sin(second)
    row = np.block([[cos2, sin2], [-sin2, cos2]]).astype(np.float32)
    row_fwd = np.concatenate(split_np(row), 0)
    row_inv = np.concatenate(split_np(np.ascontiguousarray(row.T)), 0)
    turn = np.concatenate([np.cos(twist), np.sin(twist)], 0).astype(np.float32)
    return col_fwd, col_inv, row_fwd, row_inv, turn


def mm(a, b):
    return jnp.dot(a, b, preferred_element_type=F32)


def halves(x):
    high = x.astype(BF16)
    return high, (x - high.astype(F32)).astype(BF16)


def kernel(
    geometry,
    og_any, ig_any, vi_any, sf_any, lf_any, skip_any, colf_any, coli_any, rowf_any, rowi_any, turn_any,
    out_any,
    og, ig, vi, sf, lf, skip, colf, coli, rowf, rowi, turn,
    fsend, frecv, msend, mrecv, rsend, rrecv,
    sft, toep, fil, spec, both, gate, keep, fin, outv,
    in_sem, fs_sem, fr_sem, ms_sem, mr_sem, rs_sem, rr_sem, out_sem,
):
    n_z, n_x, n_core = geometry
    n_dev = n_z * n_x * n_core
    me = lax.axis_index("ctx")
    my_z = me // (n_x * n_core)
    my_in = me % (n_x * n_core)
    my_core = me % n_core
    tokens, chans = vi.shape
    q_count = tokens // LANES
    rows = n_dev * q_count

    def peer(j):
        m = j // (n_x * n_core)
        r = (n_x * n_core) - 1 - j % (n_x * n_core)
        step = (m // 2 + 1) * (1 - 2 * ((m + my_core) % 2))
        last = m == n_z - 1
        step = jnp.where(last, 0, step)
        z = (my_z + step + n_z) % n_z
        inner = (my_in + r) % (n_x * n_core)
        return z * (n_x * n_core) + inner

    barrier = pltpu.get_barrier_semaphore()

    def hello(j, _):
        pl.semaphore_signal(barrier, inc=1, device_id={"ctx": peer(j)}, device_id_type=pl.DeviceIdType.MESH)
        return 0

    lax.fori_loop(0, n_dev - 1, hello, 0)

    loads = [
        pltpu.make_async_copy(src, dst, in_sem.at[i])
        for i, (src, dst) in enumerate(
            [
                (vi_any, vi), (ig_any, ig), (lf_any, lf), (og_any, og), (sf_any, sf), (skip_any, skip),
                (colf_any, colf), (coli_any, coli), (rowf_any, rowf), (rowi_any, rowi), (turn_any, turn),
            ]
        )
    ]
    for copy in loads:
        copy.start()

    def send_all(src, dst, ssem, rsem):
        pltpu.make_async_copy(src.at[me], dst.at[me], rsem).start()

        def go(j, _):
            p = peer(j)
            pltpu.make_async_remote_copy(
                src_ref=src.at[p],
                dst_ref=dst.at[me],
                send_sem=ssem,
                recv_sem=rsem,
                device_id={"ctx": p},
                device_id_type=pl.DeviceIdType.MESH,
            ).start()
            return 0

        lax.fori_loop(0, n_dev - 1, go, 0)

    def arrived(ref, sem):
        pltpu.make_async_copy(ref, ref, sem).wait()

    sub = lax.broadcasted_iota(jnp.int32, (LANES, LANES), 0) % OWN < HALF
    blocks = chans // LANES
    per_block = LANES // OWN

    def pick(a, b, second):
        if second:
            return jnp.where(sub, pltpu.roll(a, LANES - HALF, 0), b)
        return jnp.where(sub, a, pltpu.roll(b, HALF, 0))

    loads[2].wait()
    group = lax.broadcasted_iota(jnp.int32, (LANES, LANES), 0)
    del group
    for g in range(n_dev // 2):
        for q in range(q_count):
            row = lf[pl.ds(g, 1), q * LANES : (q + 1) * LANES]
            fsend[2 * g, pl.ds(q, 1), :] = row
            fsend[2 * g + 1, pl.ds(q, 1), :] = row

    loads[0].wait()
    loads[1].wait()
    loads[3].wait()
    for b in range(blocks):
        lanes = slice(b * LANES, (b + 1) * LANES)
        dests = slice(b * per_block, (b + 1) * per_block)
        for half in range(2):
            mixed = []
            gates = []
            for q in range(q_count):
                toks = slice(q * LANES, (q + 1) * LANES)
                v = vi[toks, lanes].astype(F32).T
                i = ig[toks, lanes].astype(F32).T
                gates.append(og[toks, lanes].astype(F32).T)
                mixed.append(pick(v, i, half).reshape(per_block, OWN, LANES))
            pairs = [
                pick(gates[q], gates[q + 1], half).reshape(per_block, OWN, LANES) for q in range(0, q_count, 2)
            ]
            packed = mixed + pairs
            for k in range(0, len(packed), 2):
                tile = jnp.concatenate([packed[k], packed[k + 1]], axis=1).astype(BF16)
                msend[half, dests, k * OWN : (k + 2) * OWN, :] = tile

    pl.semaphore_wait(barrier, n_dev - 1)
    send_all(fsend, frecv, fs_sem, fr_sem)
    for half in range(2):
        send_all(msend.at[half], mrecv.at[half], ms_sem.at[half], mr_sem.at[half])

    loads[4].wait()
    for b in range(blocks):
        sft[b * LANES : (b + 1) * LANES, :] = sf[:, b * LANES : (b + 1) * LANES].T
    taps8 = sft[pl.ds(pl.multiple_of(OWN * me, OWN), OWN), :]
    above = lax.broadcasted_iota(jnp.int32, (LANES, LANES), 1) >= lax.broadcasted_iota(jnp.int32, (LANES, LANES), 0)
    for c in range(OWN):
        row = jnp.broadcast_to(taps8[c : c + 1, :], (LANES, LANES))
        turned = pltpu.roll(row, 0, 1, stride=1, stride_axis=0)
        high, low = halves(turned)
        zero = jnp.zeros((LANES, LANES), BF16)
        toep[c, 0:LANES, 0:LANES] = jnp.where(above, high, zero)
        toep[c, LANES:, 0:LANES] = jnp.where(above, zero, high)
        toep[c, 0:LANES, LANES:] = jnp.where(above, low, zero)
        toep[c, LANES:, LANES:] = jnp.where(above, zero, low)

    for i in (5, 6, 7, 8, 9, 10):
        loads[i].wait()
    turn_re = turn[0:rows, :]
    turn_im = turn[rows:, :]

    def forward(block):
        high, low = halves(block)
        both_hl = jnp.concatenate([high, low], axis=0)
        first = mm(colf[:, 0 : 2 * rows], both_hl) + mm(colf[:, 2 * rows :], high)
        parts = []
        for k in range(block.shape[1] // LANES):
            re = first[0:rows, k * LANES : (k + 1) * LANES]
            im = first[rows:, k * LANES : (k + 1) * LANES]
            parts.append(jnp.concatenate([re * turn_re - im * turn_im, re * turn_im + im * turn_re], axis=1))
        return parts

    def along(block, table):
        high, low = halves(block)
        main = table[0 : 2 * LANES, :]
        return mm(high, main) + mm(low, main) + mm(high, table[2 * LANES :, :])

    arrived(frecv, fr_sem)
    for s in range(n_dev):
        fil[q_count * s : q_count * (s + 1), :] = frecv[s]
    scale = 1.0 / (rows * LANES)
    spec[...] = along(forward(fil[...])[0], rowf) * scale

    for half in range(2):
        arrived(mrecv.at[half], mr_sem.at[half])
        data = mrecv[half]
        main = q_count * OWN
        both[...] = data[:, 0:main, :].astype(F32).reshape(rows * OWN, LANES)
        gate[...] = data[:, main:, :].astype(F32).reshape(rows * HALF, LANES)
        spectra = []
        for pair in range(2):
            gated = []
            for c in (2 * pair, 2 * pair + 1):
                v = both[pl.ds(c, rows, stride=OWN), :]
                i = both[pl.ds(HALF + c, rows, stride=OWN), :]
                line = lax.broadcasted_iota(jnp.int32, (rows, LANES), 0)
                before = jnp.where(line == 0, 0.0, pltpu.roll(v, 1, 0))
                taken = jnp.concatenate([v.astype(BF16), before.astype(BF16)], axis=1)
                short = mm(taken, toep[half * HALF + c])
                gated.append(i * (short[:, 0:LANES] + short[:, LANES:]))
            block = jnp.concatenate(gated, axis=1)
            keep[pair] = block
            spectra += forward(block)
        stacked = along(jnp.concatenate(spectra, axis=0), rowf)
        prods = []
        h_re = spec[:, 0:LANES]
        h_im = spec[:, LANES:]
        for c in range(HALF):
            re = stacked[c * rows : (c + 1) * rows, 0:LANES]
            im = stacked[c * rows : (c + 1) * rows, LANES:]
            prods.append(jnp.concatenate([re * h_re - im * h_im, re * h_im + im * h_re], axis=1))
        back = along(jnp.concatenate(prods, axis=0), rowi)
        for pair in range(2):
            reals = []
            imags = []
            for c in (2 * pair, 2 * pair + 1):
                re = back[c * rows : (c + 1) * rows, 0:LANES]
                im = back[c * rows : (c + 1) * rows, LANES:]
                reals.append(re * turn_re + im * turn_im)
                imags.append(im * turn_re - re * turn_im)
            block = jnp.concatenate([jnp.concatenate(reals, axis=1), jnp.concatenate(imags, axis=1)], axis=0)
            high, low = halves(block)
            wide = mm(coli[...], high)
            result = wide[0:rows] + wide[rows:] + mm(coli[0:rows, :], low)
            for k in range(2):
                c = 2 * pair + k
                lanes = slice(k * LANES, (k + 1) * LANES)
                gain = skip[half * HALF + c + OWN * me]
                total = result[:, lanes] + gain * keep[pair, :, lanes]
                fin[pl.ds(c, rows, stride=HALF), :] = gate[pl.ds(c, rows, stride=HALF), :] * total
        rsend[half] = fin[...].reshape(n_dev, q_count * HALF, LANES).astype(BF16)
        send_all(rsend.at[half], rrecv.at[half], rs_sem.at[half], rr_sem.at[half])

    arrived(rrecv.at[0], rr_sem.at[0])
    arrived(rrecv.at[1], rr_sem.at[1])
    for b in range(blocks):
        dests = slice(b * per_block, (b + 1) * per_block)
        lanes = slice(b * LANES, (b + 1) * LANES)
        first = rrecv[0, dests].astype(F32)
        second = rrecv[1, dests].astype(F32)
        for k in range(q_count // 2):
            a = first[:, k * OWN : (k + 1) * OWN, :].reshape(LANES, LANES)
            c = second[:, k * OWN : (k + 1) * OWN, :].reshape(LANES, LANES)
            outv[2 * k * LANES : (2 * k + 1) * LANES, lanes] = pick(a, c, 0).T.astype(BF16)
            outv[(2 * k + 1) * LANES : (2 * k + 2) * LANES, lanes] = pick(a, c, 1).T.astype(BF16)
    done = pltpu.make_async_copy(outv, out_any, out_sem)
    done.start()
    sent = n_dev - 1
    arrived(fsend.at[pl.ds(0, sent)], fs_sem)
    for half in range(2):
        arrived(msend.at[half, pl.ds(0, sent)], ms_sem.at[half])
        arrived(rsend.at[half, pl.ds(0, sent)], rs_sem.at[half])
    done.wait()


def local(geometry, output_gate, input_gate, value_input, short_filter, long_filter, skip_gain):
    n_dev = math.prod(geometry)
    tokens, chans = value_input.shape
    q_count = tokens // LANES
    rows = n_dev * q_count
    tabs = [jnp.asarray(t) for t in tables(rows)]
    operands = [output_gate, input_gate, value_input, short_filter, long_filter.T, skip_gain] + tabs
    message = q_count * (OWN + HALF)
    scratch = [pltpu.VMEM(x.shape, x.dtype) for x in operands]
    scratch[5] = pltpu.SMEM(skip_gain.shape, F32)
    scratch += [
        pltpu.VMEM((n_dev, q_count, LANES), F32),
        pltpu.VMEM((n_dev, q_count, LANES), F32),
        pltpu.VMEM((2, n_dev, message, LANES), BF16),
        pltpu.VMEM((2, n_dev, message, LANES), BF16),
        pltpu.VMEM((2, n_dev, q_count * HALF, LANES), BF16),
        pltpu.VMEM((2, n_dev, q_count * HALF, LANES), BF16),
        pltpu.VMEM((chans, LANES), F32),
        pltpu.VMEM((OWN, 2 * LANES, 2 * LANES), BF16),
        pltpu.VMEM((rows, LANES), F32),
        pltpu.VMEM((rows, 2 * LANES), F32),
        pltpu.VMEM((rows * OWN, LANES), F32),
        pltpu.VMEM((rows * HALF, LANES), F32),
        pltpu.VMEM((2, rows, 2 * LANES), F32),
        pltpu.VMEM((rows * HALF, LANES), F32),
        pltpu.VMEM((tokens, chans), BF16),
        pltpu.SemaphoreType.DMA((len(operands),)),
        pltpu.SemaphoreType.DMA,
        pltpu.SemaphoreType.DMA,
        pltpu.SemaphoreType.DMA((2,)),
        pltpu.SemaphoreType.DMA((2,)),
        pltpu.SemaphoreType.DMA((2,)),
        pltpu.SemaphoreType.DMA((2,)),
        pltpu.SemaphoreType.DMA,
    ]
    return pl.pallas_call(
        functools.partial(kernel, geometry),
        out_shape=jax.ShapeDtypeStruct((tokens, chans), BF16),
        in_specs=[pl.BlockSpec(memory_space=pl.ANY)] * len(operands),
        out_specs=pl.BlockSpec(memory_space=pl.ANY),
        scratch_shapes=scratch,
        compiler_params=pltpu.CompilerParams(collective_id=0, has_side_effects=True, vmem_limit_bytes=48 << 20),
    )(*operands)


def solution(mesh):
    placed = (
        P("ctx", "ch"),
        P("ctx", "ch"),
        P("ctx", "ch"),
        P(None, "ch"),
        P("ctx", "ch"),
        P("ch"),
    )
    n_ctx = mesh.shape["ctx"]
    geometry = (n_ctx // 4, 2, 2)
    return jax.shard_map(
        functools.partial(local, geometry), mesh=mesh, in_specs=placed, out_specs=P("ctx", "ch"), check_vma=False
    )
```

time: 105 us -> 57 us (0.54)
  Pallas kernels: 0 us -> 46 us
  matrix products: 36.3 us -> 0 us
  starting transfers between devices: 25.1 us -> 0 us
  blocking collectives: 22.5 us -> 0 us
  waiting for transfers between devices: 11.1 us -> 0 us
  local copies, waits for them, and re-layouts: 6.17 us -> 10.5 us
  other arithmetic: 2.53 us -> 0 us
    pallas_call x0 -> x1, Pallas kernels: none -> 46 us  [local(): pl.pallas_call(functools.partial(kernel, geometry), out_shape=jax.ShapeDt...]
    dot_general x22 -> x0, matrix products: 24.8 us -> none  [the longest x5 6.23 us: table_apply(): jnp.einsum(pattern, cosine, imag_part, precision=HIGHEST)]
    all_to_all x1 -> x0, blocking collectives: 22.5 us -> none  [local(): lax.all_to_all(convolved, 'ctx', split_axis=0, concat_axis=1, tiled=True)]
    all_to_all x2 -> x0, starting transfers between devices: 19.1 us -> none  [the longest x1 11.4 us: local(): lax.all_to_all(widened, 'ctx', split_axis=1, concat_axis=0, tiled=True)]
    conv_general_dilated x1 -> x0, matrix products: 11.6 us -> none  [depthwise(): lax.conv_general_dilated(extended[None], kernel, (1,), 'VALID', dimension...]
    all_to_all x2 -> x0, waiting for transfers between devices: 11.1 us -> none  [the longest x1 8.76 us: local(): lax.all_to_all(gated, 'ctx', split_axis=1, concat_axis=0, tiled=True)]
    unnamed x20 -> x23, local copies, waits for them, and re-layouts: 1.83 us -> 10.5 us
    ppermute x1 -> x0, starting transfers between devices: 6.03 us -> none  [passed_along(): return lax.ppermute(block, axis, route)]
  transfers between devices with their start and end apart: 3 -> 0, of which waited for: 2 -> 0; matrix products, arithmetic and copies ran while one was open for 22% -> 0% of each run, Pallas kernels for 0% -> 0%
where the time goes in v1:
time: 57 us; the launch traced here: 56.6 us
  Pallas kernels  46 us (81%)
  local copies, waits for them, and re-layouts  10.5 us (18%)
    pallas_call x1, Pallas kernels, local(): pl.pallas_call(functools.partial(kernel, geometry), out_shape=jax.ShapeDt...  46 us
    unnamed x23, local copies, waits for them, and re-layouts  10.5 us

profile of v1, /device:TPU:1, one launch (start us, length us, event | category | flops | bytes accessed | tf_op | source)
XLA Modules:
  0.0 56.6 jit_solution(14845562355125192381)
XLA Ops:
  0.0 0.0 copy-start.10
  0.0 0.7 %copy-done.10 = f32[256]{0:T(256)S(1)} copy-done((f32[256]{0:T(256)S(1)}, f32[256]{0:T(256)}, u32[]{:S(2)}) %copy-start.10) | copy-done | bytes 1048
  0.7 0.0 copy-start
  0.7 0.9 %copy-done = bf16[512,256]{1,0:T(8,128)(2,1)S(1)} copy-done((bf16[512,256]{1,0:T(8,128)(2,1)S(1)}, bf16[512,256]{1,0:T(8,128)(2,1)}, u32[]{:S(2)}) %copy-start) | copy-done | bytes 262168
  1.6 0.0 copy-start.1
  1.6 0.9 %copy-done.1 = bf16[512,256]{1,0:T(8,128)(2,1)S(1)} copy-done((bf16[512,256]{1,0:T(8,128)(2,1)S(1)}, bf16[512,256]{1,0:T(8,128)(2,1)}, u32[]{:S(2)}) %copy-start.1) | copy-done | bytes 262168
  2.6 0.0 copy-start.2
  2.6 0.9 %copy-done.2 = bf16[512,256]{1,0:T(8,128)(2,1)S(1)} copy-done((bf16[512,256]{1,0:T(8,128)(2,1)S(1)}, bf16[512,256]{1,0:T(8,128)(2,1)}, u32[]{:S(2)}) %copy-start.2) | copy-done | bytes 262168
  3.5 0.0 copy-start.3
  3.5 0.9 %copy-done.3 = bf16[512,256]{1,0:T(8,128)(2,1)S(1)} copy-done((bf16[512,256]{1,0:T(8,128)(2,1)S(1)}, bf16[512,256]{1,0:T(8,128)(2,1)}, u32[]{:S(2)}) %copy-start.3) | copy-done | bytes 262168
  4.5 0.0 copy-start.4
  4.5 0.9 %copy-done.4 = bf16[512,256]{1,0:T(8,128)(2,1)S(1)} copy-done((bf16[512,256]{1,0:T(8,128)(2,1)S(1)}, bf16[512,256]{1,0:T(8,128)(2,1)}, u32[]{:S(2)}) %copy-start.4) | copy-done | bytes 262168
  5.4 0.0 copy-start.5
  5.4 0.9 %copy-done.5 = bf16[256,384]{1,0:T(8,128)(2,1)S(1)} copy-done((bf16[256,384]{1,0:T(8,128)(2,1)S(1)}, bf16[256,384]{1,0:T(8,128)(2,1)}, u32[]{:S(2)}) %copy-start.5) | copy-done | bytes 196632
  6.4 0.0 copy-start.6
  6.4 0.9 %copy-done.6 = f32[128,256]{1,0:T(8,128)S(1)} copy-done((f32[128,256]{1,0:T(8,128)S(1)}, f32[128,256]{1,0:T(8,128)}, u32[]{:S(2)}) %copy-start.6) | copy-done | bytes 131096
  7.3 0.0 copy-start.7
  7.3 0.9 %copy-done.7 = f32[256,128]{1,0:T(8,128)S(1)} copy-done((f32[256,128]{1,0:T(8,128)S(1)}, f32[256,128]{1,0:T(8,128)}, u32[]{:S(2)}) %copy-start.7) | copy-done | bytes 131096
  8.2 0.0 copy-start.8
  8.2 0.9 %copy-done.8 = bf16[256,256]{1,0:T(8,128)(2,1)S(1)} copy-done((bf16[256,256]{1,0:T(8,128)(2,1)S(1)}, bf16[256,256]{1,0:T(8,128)(2,1)}, u32[]{:S(2)}) %copy-start.8) | copy-done | bytes 131096
  9.1 0.0 copy-start.9
  9.1 0.8 %copy-done.9 = f32[512,16]{0,1:T(8,128)S(1)} copy-done((f32[512,16]{0,1:T(8,128)S(1)}, f32[512,16]{0,1:T(8,128)}, u32[]{:S(2)}) %copy-start.9) | copy-done | bytes 32792
  9.8 46.0 %shard_map.109 = bf16[512,256]{1,0:T(8,128)(2,1)S(1)} custom-call(bf16[512,256]{1,0:T(8,128)(2,1)S(1)} %copy-done, bf16[512,256]{1,0:T(8,128)(2,1)S(1)} %copy-done.1, bf16[512,256]{1,0:T(8,128)(2,1)S(1)} %copy-done.2, f32[128,256]{1,0:T(8,128)S(1)} %copy-done.6, f32[16,512]{1,0:T(8,128)S(1)} %bitcast.1, f32[256]{0:T(256)S(1)} %copy-done.10, ...), custom_call_target="tpu_custom_call" | custom-call | tf_op jit(solution)/shard_map/pallas_call | solution.py:319
  55.9 0.7 %copy.13 = bf16[512,256]{1,0:T(8,128)(2,1)} copy(bf16[512,256]{1,0:T(8,128)(2,1)S(1)} %shard_map.109) | data formatting | bytes 524288
Async XLA Ops:
  0.0 0.7 %copy-start.10 = (f32[256]{0:T(256)S(1)}, f32[256]{0:T(256)}, u32[]{:S(2)}) copy-start(f32[256]{0:T(256)} %skip_any.1) | copy-start | bytes 3076
  0.7 0.9 %copy-start = (bf16[512,256]{1,0:T(8,128)(2,1)S(1)}, bf16[512,256]{1,0:T(8,128)(2,1)}, u32[]{:S(2)}) copy-start(bf16[512,256]{1,0:T(8,128)(2,1)} %og_any.1) | copy-start | bytes 786436
  1.6 0.9 %copy-start.1 = (bf16[512,256]{1,0:T(8,128)(2,1)S(1)}, bf16[512,256]{1,0:T(8,128)(2,1)}, u32[]{:S(2)}) copy-start(bf16[512,256]{1,0:T(8,128)(2,1)} %ig_any.1) | copy-start | bytes 786436
  2.6 0.9 %copy-start.2 = (bf16[512,256]{1,0:T(8,128)(2,1)S(1)}, bf16[512,256]{1,0:T(8,128)(2,1)}, u32[]{:S(2)}) copy-start(bf16[512,256]{1,0:T(8,128)(2,1)} %vi_any.1) | copy-start | bytes 786436
  3.5 0.9 %copy-start.3 = (bf16[512,256]{1,0:T(8,128)(2,1)S(1)}, bf16[512,256]{1,0:T(8,128)(2,1)}, u32[]{:S(2)}) copy-start(bf16[512,256]{1,0:T(8,128)(2,1)} %constant.13.clone.rowi_any) | copy-start | bytes 786436
  4.5 0.9 %copy-start.4 = (bf16[512,256]{1,0:T(8,128)(2,1)S(1)}, bf16[512,256]{1,0:T(8,128)(2,1)}, u32[]{:S(2)}) copy-start(bf16[512,256]{1,0:T(8,128)(2,1)} %constant.12.clone.rowf_any) | copy-start | bytes 786436
  5.4 0.9 %copy-start.5 = (bf16[256,384]{1,0:T(8,128)(2,1)S(1)}, bf16[256,384]{1,0:T(8,128)(2,1)}, u32[]{:S(2)}) copy-start(bf16[256,384]{1,0:T(8,128)(2,1)} %constant.10.clone.colf_any) | copy-start | bytes 589828
  6.4 0.9 %copy-start.6 = (f32[128,256]{1,0:T(8,128)S(1)}, f32[128,256]{1,0:T(8,128)}, u32[]{:S(2)}) copy-start(f32[128,256]{1,0:T(8,128)} %sf_any.1) | copy-start | bytes 393220
  7.3 0.9 %copy-start.7 = (f32[256,128]{1,0:T(8,128)S(1)}, f32[256,128]{1,0:T(8,128)}, u32[]{:S(2)}) copy-start(f32[256,128]{1,0:T(8,128)} %constant.14.clone.turn_any) | copy-start | bytes 393220
  8.2 0.9 %copy-start.8 = (bf16[256,256]{1,0:T(8,128)(2,1)S(1)}, bf16[256,256]{1,0:T(8,128)(2,1)}, u32[]{:S(2)}) copy-start(bf16[256,256]{1,0:T(8,128)(2,1)} %constant.11.clone.coli_any) | copy-start | bytes 393220
  9.1 0.8 %copy-start.9 = (f32[512,16]{0,1:T(8,128)S(1)}, f32[512,16]{0,1:T(8,128)}, u32[]{:S(2)}) copy-start(f32[512,16]{0,1:T(8,128)} %param.15) | copy-start | bytes 98308

commit v2 on v0

v2 whole, which is shorter than its diff:
```python
import functools
import math

import jax
import jax.numpy as jnp
import numpy as np
from jax import lax
from jax.experimental import pallas as pl
from jax.experimental.pallas import tpu as pltpu
from jax.sharding import PartitionSpec as P

LANES = 128
OWN = 8
INNER = 4
F32 = jnp.float32
BF16 = jnp.bfloat16
MESH = pl.DeviceIdType.MESH
KNEE = 64.0
SPAN = 120.0
POWER = 2 * SPAN / math.log2(1 + KNEE)


def split_np(table):
    table = table.astype(np.float32)
    high = table.astype(BF16)
    low = (table - high.astype(np.float32)).astype(BF16)
    return high, low


def long_tables(rows):
    length = rows * LANES
    n1 = np.arange(rows)
    n2 = np.arange(LANES)
    first = np.pi * n1[None, :] * LANES / (2 * length) - 2 * np.pi * ((n1[:, None] * n1[None, :]) % rows) / rows
    twist = np.pi * n2[None, :] / (2 * length) - 2 * np.pi * ((n1[:, None] * n2[None, :]) % length) / length
    second = -2 * np.pi * ((n2[:, None] * n2[None, :]) % LANES) / LANES
    hi, lo = split_np(np.concatenate([np.cos(first), np.sin(first)], 0))
    col_fwd = np.concatenate([hi, hi, lo], 1)
    cos1, sin1 = np.cos(first).T, np.sin(first).T
    hi, lo = split_np(np.block([[cos1, sin1], [-sin1, cos1]]))
    col_inv = np.concatenate([hi, hi, lo], 1)
    cos2, sin2 = np.cos(second), np.sin(second)
    row = np.block([[cos2, sin2], [-sin2, cos2]])
    row_fwd = np.concatenate(split_np(row), 0)
    row_inv = np.concatenate(split_np(row.T), 0)
    turn = np.concatenate([np.cos(twist), np.sin(twist)], 0).astype(np.float32)
    return col_fwd, col_inv, row_fwd, row_inv, turn


def short_tables():
    size = 2 * LANES
    n = np.arange(size)
    k = np.arange(LANES)
    angle = 2 * np.pi * ((n[:, None] * k[None, :]) % size) / size
    re, im = np.cos(angle), -np.sin(angle)
    im[:, 0] = np.where(n % 2 == 0, 1.0, -1.0)
    fwd = np.concatenate(split_np(np.concatenate([re, im], 1)), 0)
    weight = np.where(k == 0, 1.0, 2.0) / size
    back = np.concatenate([(re * weight).T, (im * weight).T], 0)[:, LANES:]
    inv = np.concatenate(split_np(back), 1)
    return fwd, inv


def mm(a, b):
    return jnp.dot(a, b, preferred_element_type=F32)


def halves(x):
    high = x.astype(BF16)
    return high, (x - high.astype(F32)).astype(BF16)


def peak(x):
    top = jnp.max(jnp.max(jnp.abs(x), axis=0, keepdims=True), axis=1, keepdims=True)
    return jnp.broadcast_to(jnp.maximum(top, 1e-30), (1, LANES))


def encode(x, top):
    size = jnp.exp2(POWER * jnp.log2(1.0 + jnp.abs(x) * (KNEE / top)) - SPAN)
    return jnp.where(x < 0, -size, size)


def decode(code, top):
    size = (jnp.exp2((jnp.log2(jnp.abs(code)) + SPAN) * (1.0 / POWER)) - 1.0) * (top * (1.0 / KNEE))
    return jnp.where(code < 0, -size, size)


def along(block, table):
    high, low = halves(block)
    main = table[0 : 2 * LANES, :]
    return mm(high, main) + mm(low, main) + mm(high, table[2 * LANES :, :])


def kernel(
    n_z,
    og_any, ig_any, vi_any, sf_any, lf_any, skip_any, colf_any, coli_any, rowf_any, rowi_any, turn_any, shf_any, shi_any,
    out_any,
    og, ig, vi, sf, lf, skip, colf, coli, rowf, rowi, turn, shf, shi,
    halo, vt, igt, skipt, taps, keep, fsend, frecv, msend, mrecv, tsend, trecv, rsend, rrecv, usend, urecv,
    spec, xs, cross, carry, fin, outv,
    in_sem, halo_sem, fs_sem, fr_sem, ms_sem, mr_sem, ts_sem, tr_sem, rs_sem, rr_sem, us_sem, ur_sem, out_sem,
):
    n_dev = n_z * INNER
    half_z = n_z // 2
    half_dev = n_dev // 2
    me = lax.axis_index("ctx")
    my_z = me // INNER
    my_in = me % INNER
    my_core = me % 2
    my_half = me // half_dev
    tokens, chans = vi.shape
    q_count = tokens // LANES
    rows = half_dev * q_count
    blocks = chans // LANES
    per_block = LANES // OWN

    inners = [(my_in + r) % INNER for r in range(INNER)]
    turns = []
    for d in range(1, n_z // 2):
        turns += [d, -d]
    turns += [n_z // 2, 0]
    sign = 1 - 2 * my_core
    planes = [((my_z + sign * d + n_z) % n_z) * INNER for d in turns]
    peers = [z + i for z in planes for i in inners[1:] + inners[:1]][:-1]

    barrier = pltpu.get_barrier_semaphore()
    for p in peers:
        pl.semaphore_signal(barrier, inc=1, device_id={"ctx": p}, device_id_type=MESH)

    order = [
        (vi_any, vi), (ig_any, ig), (shf_any, shf), (sf_any, sf), (lf_any, lf), (shi_any, shi), (og_any, og), (skip_any, skip),
        (colf_any, colf), (coli_any, coli), (rowf_any, rowf), (rowi_any, rowi), (turn_any, turn),
    ]
    loads = [pltpu.make_async_copy(src, dst, in_sem.at[i]) for i, (src, dst) in enumerate(order)]
    for copy in loads:
        copy.start()

    def remote(src, dst, ssem, rsem, p):
        pltpu.make_async_remote_copy(
            src_ref=src, dst_ref=dst, send_sem=ssem, recv_sem=rsem, device_id={"ctx": p}, device_id_type=MESH
        ).start()

    def arrived(ref, sem):
        pltpu.make_async_copy(ref, ref, sem).wait()

    def send_all(src_of, dst, ssem, rsem):
        pltpu.make_async_copy(src_of(me), dst.at[me], rsem).start()
        for p in peers:
            remote(src_of(p), dst.at[me], ssem, rsem, p)

    def put_block(b, q):
        toks = slice(q * LANES, (q + 1) * LANES)
        lanes = slice(b * LANES, (b + 1) * LANES)
        vt[q + 1, lanes, :] = vi[toks, lanes].astype(F32).T.astype(BF16)
        igt[q, lanes, :] = ig[toks, lanes].astype(F32).T

    loads[0].wait()
    loads[1].wait()
    for q in range(q_count):
        for b in range(blocks):
            put_block(b, q)

    loads[2].wait()
    loads[3].wait()
    lane = lax.broadcasted_iota(jnp.int32, (LANES, LANES), 1)
    for b in range(blocks):
        lanes = slice(b * LANES, (b + 1) * LANES)
        high, low = halves(sf[:, lanes].T)
        upper = shf[0:LANES, :]
        freq = mm(high, upper) + mm(low, upper) + mm(high, shf[2 * LANES : 3 * LANES, :])
        f_re, f_im = freq[:, 0:LANES], freq[:, LANES:]
        taps[0, lanes, :] = f_re
        taps[1, lanes, :] = jnp.where(lane == 0, 0.0, f_im)
        taps[2, lanes, :] = jnp.where(lane == 0, f_im, f_re)

    loads[4].wait()
    for g in range(n_dev // 2):
        for q in range(q_count):
            fsend[g, pl.ds(q, 1), :] = lf[pl.ds(g, 1), q * LANES : (q + 1) * LANES]
    loads[5].wait()

    def short(q):
        for b in range(blocks):
            lanes = slice(b * LANES, (b + 1) * LANES)
            window = jnp.concatenate([vt[q, lanes, :], vt[q + 1, lanes, :]], axis=1)
            freq = mm(window, shf[0 : 2 * LANES, :]) + mm(window, shf[2 * LANES :, :])
            re, im = freq[:, 0:LANES], freq[:, LANES:]
            f_re, f_zero, f_top = taps[0, lanes, :], taps[1, lanes, :], taps[2, lanes, :]
            prod = jnp.concatenate([re * f_re - im * f_zero, re * f_zero + im * f_top], axis=1)
            high, low = halves(prod)
            wide = mm(high, shi[...])
            keep[q, lanes, :] = igt[q, lanes, :] * (wide[:, 0:LANES] + wide[:, LANES:] + mm(low, shi[:, 0:LANES]))

    def pack(part):
        q = 2 * part
        top = peak(keep[q : q + 2].reshape(2 * chans, LANES))
        tsend[part] = top
        first = encode(keep[q], top).reshape(n_dev, OWN, LANES)
        second = encode(keep[q + 1], top).reshape(n_dev, OWN, LANES)
        msend[part] = jnp.concatenate([first, second], axis=1).astype(BF16)

    parts = q_count // 2
    for q in range(q_count - 1, 0, -1):
        short(q)
    for part in range(parts - 1, 0, -1):
        pack(part)

    pl.semaphore_wait(barrier, n_dev - 1)
    remote(vi.at[tokens - LANES :, :], halo, halo_sem.at[0], halo_sem.at[1], (me + 1) % n_dev)
    send_all(lambda p: fsend.at[p // 2], frecv, fs_sem, fr_sem)

    def send_part(part):
        send_all(lambda p: msend.at[part, p], mrecv.at[part], ms_sem.at[part], mr_sem.at[part, my_half])
        send_all(lambda p: tsend.at[part], trecv.at[part], ts_sem.at[part], tr_sem.at[part, my_half])

    for part in range(parts - 1, 0, -1):
        send_part(part)

    pltpu.make_async_copy(halo, halo, halo_sem.at[1]).wait()
    for b in range(blocks):
        lanes = slice(b * LANES, (b + 1) * LANES)
        before = halo[:, lanes].astype(F32).T
        vt[0, lanes, :] = jnp.where(me > 0, before, 0.0).astype(BF16)
    short(0)
    pack(0)
    send_part(0)

    for i in range(6, len(order)):
        loads[i].wait()
    for b in range(blocks):
        lanes = slice(b * LANES, (b + 1) * LANES)
        skipt[lanes, :] = jnp.broadcast_to(skip[:, lanes], (LANES, LANES)).T

    turn_re = turn[0:rows, :]
    turn_im = turn[rows:, :]

    def forward(block):
        high, low = halves(block)
        first = mm(colf[...], jnp.concatenate([high, low, high], axis=0))
        pieces = []
        for k in range(block.shape[1] // LANES):
            re = first[0:rows, k * LANES : (k + 1) * LANES]
            im = first[rows:, k * LANES : (k + 1) * LANES]
            pieces.append(jnp.concatenate([re * turn_re - im * turn_im, re * turn_im + im * turn_re], axis=1))
        return along(jnp.concatenate(pieces, axis=0), rowf[...])

    def backward(block, keep_rows):
        mid = along(block, rowi[...])
        reals, imags = [], []
        for c in range(OWN):
            re = mid[c * rows : (c + 1) * rows, 0:LANES]
            im = mid[c * rows : (c + 1) * rows, LANES:]
            reals.append(re * turn_re + im * turn_im)
            imags.append(im * turn_re - re * turn_im)
        high, low = halves(jnp.concatenate([jnp.concatenate(reals, axis=1), jnp.concatenate(imags, axis=1)], axis=0))
        return mm(coli[0:keep_rows, :], jnp.concatenate([high, low, high], axis=0))

    def times(spectra, which):
        h_re = spec[which, :, 0:LANES]
        h_im = spec[which, :, LANES:]
        out = []
        for c in range(OWN):
            re = spectra[c * rows : (c + 1) * rows, 0:LANES]
            im = spectra[c * rows : (c + 1) * rows, LANES:]
            out.append(jnp.concatenate([re * h_re - im * h_im, re * h_im + im * h_re], axis=1))
        return jnp.concatenate(out, axis=0)

    arrived(frecv, fr_sem)
    for s in range(n_dev):
        which, at = s // half_dev, s % half_dev
        fin[q_count * at : q_count * (at + 1), which * LANES : (which + 1) * LANES] = frecv[s]
    both = forward(fin[...]) * (1.0 / (rows * LANES))
    spec[0] = both[0:rows]
    spec[1] = both[rows:]

    def owned(half):
        span = pl.ds(half * half_dev, half_dev)
        got = []
        for part in range(parts):
            arrived(mrecv.at[part, span], mr_sem.at[part, half])
            arrived(trecv.at[part, span], tr_sem.at[part, half])
            got.append(decode(mrecv[part, span].astype(F32), trecv[part, span]))
        xs[...] = jnp.concatenate(got, axis=1).reshape(rows * OWN, LANES)
        return jnp.concatenate([xs[pl.ds(c, rows, stride=OWN), :] for c in range(OWN)], axis=1)

    def give_back(half, result):
        top = peak(result)
        usend[half] = top
        wide = jnp.concatenate([top] * OWN, axis=1)
        code = encode(result, wide)
        for c in range(OWN):
            xs[pl.ds(c, rows, stride=OWN), :] = code[:, c * LANES : (c + 1) * LANES]
        rsend[half] = xs[...].reshape(half_dev, q_count * OWN, LANES).astype(BF16)
        for k in range(half_z):
            z = (my_z + k) % half_z
            for r in range(INNER):
                at = z * INNER + inners[r]
                p = half * half_dev + at

                def away():
                    remote(rsend.at[half, at], rrecv.at[me], rs_sem, rr_sem, p)
                    remote(usend.at[half], urecv.at[me], us_sem, ur_sem, p)

                if k or r:
                    away()
                else:
                    pl.when(my_half != half)(away)

                    @pl.when(my_half == half)
                    def _():
                        pltpu.make_async_copy(rsend.at[half, at], rrecv.at[me], rr_sem).start()
                        pltpu.make_async_copy(usend.at[half], urecv.at[me], ur_sem).start()

    spectra = forward(owned(0))
    result = backward(times(spectra, 0), 2 * rows)
    carry[...] = result[rows:]
    give_back(0, result[0:rows])
    cross[...] = times(spectra, 1)
    spectra = forward(owned(1))
    give_back(1, backward(times(spectra, 0) + cross[...], rows) + carry[...])

    arrived(rrecv, rr_sem)
    arrived(urecv, ur_sem)
    for q in range(q_count):
        toks = slice(q * LANES, (q + 1) * LANES)
        code = rrecv[:, (q // 2) * 2 * OWN : (q // 2 + 1) * 2 * OWN, :].astype(F32)[:, (q % 2) * OWN : (q % 2 + 1) * OWN, :]
        total = decode(code, urecv[...]).reshape(chans, LANES) + skipt[...] * keep[q]
        for b in range(blocks):
            lanes = slice(b * LANES, (b + 1) * LANES)
            outv[toks, lanes] = (og[toks, lanes].astype(F32) * total[lanes, :].T).astype(BF16)
    done = pltpu.make_async_copy(outv, out_any, out_sem)
    done.start()

    sent = pl.ds(0, n_dev - 1)
    arrived(halo, halo_sem.at[0])
    arrived(frecv.at[sent], fs_sem)
    for part in range(parts):
        arrived(mrecv.at[part, sent], ms_sem.at[part])
        arrived(trecv.at[part, sent], ts_sem.at[part])
    arrived(rrecv.at[sent], rs_sem)
    arrived(urecv.at[sent], us_sem)
    done.wait()


def local(n_z, output_gate, input_gate, value_input, short_filter, long_filter, skip_gain):
    n_dev = n_z * INNER
    tokens, chans = value_input.shape
    q_count = tokens // LANES
    parts = q_count // 2
    rows = n_dev * q_count // 2
    tabs = [jnp.asarray(t) for t in long_tables(rows) + short_tables()]
    operands = [output_gate, input_gate, value_input, short_filter, long_filter.T, skip_gain.reshape(1, chans)] + tabs
    dma = pltpu.SemaphoreType.DMA
    scratch = [pltpu.VMEM(x.shape, x.dtype) for x in operands]
    scratch += [
        pltpu.VMEM((LANES, chans), BF16),
        pltpu.VMEM((q_count + 1, chans, LANES), BF16),
        pltpu.VMEM((q_count, chans, LANES), F32),
        pltpu.VMEM((chans, LANES), F32),
        pltpu.VMEM((3, chans, LANES), F32),
        pltpu.VMEM((q_count, chans, LANES), F32),
        pltpu.VMEM((n_dev // 2, q_count, LANES), F32),
        pltpu.VMEM((n_dev, q_count, LANES), F32),
        pltpu.VMEM((parts, n_dev, 2 * OWN, LANES), BF16),
        pltpu.VMEM((parts, n_dev, 2 * OWN, LANES), BF16),
        pltpu.VMEM((parts, 1, LANES), F32),
        pltpu.VMEM((parts, n_dev, 1, LANES), F32),
        pltpu.VMEM((2, n_dev // 2, q_count * OWN, LANES), BF16),
        pltpu.VMEM((n_dev, q_count * OWN, LANES), BF16),
        pltpu.VMEM((2, 1, LANES), F32),
        pltpu.VMEM((n_dev, 1, LANES), F32),
        pltpu.VMEM((2, rows, 2 * LANES), F32),
        pltpu.VMEM((rows * OWN, LANES), F32),
        pltpu.VMEM((rows * OWN, 2 * LANES), F32),
        pltpu.VMEM((rows, OWN * LANES), F32),
        pltpu.VMEM((rows, 2 * LANES), F32),
        pltpu.VMEM((tokens, chans), BF16),
        dma((len(operands),)), dma((2,)), dma, dma, dma((parts,)), dma((parts, 2)), dma((parts,)), dma((parts, 2)),
        dma, dma, dma, dma, dma,
    ]
    return pl.pallas_call(
        functools.partial(kernel, n_z),
        out_shape=jax.ShapeDtypeStruct((tokens, chans), BF16),
        in_specs=[pl.BlockSpec(memory_space=pl.ANY)] * len(operands),
        out_specs=pl.BlockSpec(memory_space=pl.ANY),
        scratch_shapes=scratch,
        compiler_params=pltpu.CompilerParams(collective_id=0, has_side_effects=True, vmem_limit_bytes=60 << 20),
    )(*operands)


def solution(mesh):
    placed = (
        P("ctx", "ch"),
        P("ctx", "ch"),
        P("ctx", "ch"),
        P(None, "ch"),
        P("ctx", "ch"),
        P("ch"),
    )
    n_z = mesh.shape["ctx"] // INNER
    return jax.shard_map(
        functools.partial(local, n_z), mesh=mesh, in_specs=placed, out_specs=P("ctx", "ch"), check_vma=False
    )
```

time: 105 us -> 40.4 us (0.38)
  Pallas kernels: 0 us -> 38.6 us
  matrix products: 36.3 us -> 0 us
  starting transfers between devices: 25.1 us -> 0 us
  blocking collectives: 22.5 us -> 0 us
  waiting for transfers between devices: 11.1 us -> 0 us
  local copies, waits for them, and re-layouts: 6.17 us -> 1.67 us
  other arithmetic: 2.53 us -> 0 us
    pallas_call x0 -> x1, Pallas kernels: none -> 38.6 us  [local(): pl.pallas_call(functools.partial(kernel, n_z), out_shape=jax.ShapeDtypeSt...]
    dot_general x22 -> x0, matrix products: 24.8 us -> none  [the longest x5 6.23 us: table_apply(): jnp.einsum(pattern, cosine, imag_part, precision=HIGHEST)]
    all_to_all x1 -> x0, blocking collectives: 22.5 us -> none  [local(): lax.all_to_all(convolved, 'ctx', split_axis=0, concat_axis=1, tiled=True)]
    all_to_all x2 -> x0, starting transfers between devices: 19.1 us -> none  [the longest x1 11.4 us: local(): lax.all_to_all(widened, 'ctx', split_axis=1, concat_axis=0, tiled=True)]
    conv_general_dilated x1 -> x0, matrix products: 11.6 us -> none  [depthwise(): lax.conv_general_dilated(extended[None], kernel, (1,), 'VALID', dimension...]
    all_to_all x2 -> x0, waiting for transfers between devices: 11.1 us -> none  [the longest x1 8.76 us: local(): lax.all_to_all(gated, 'ctx', split_axis=1, concat_axis=0, tiled=True)]
    ppermute x1 -> x0, starting transfers between devices: 6.03 us -> none  [passed_along(): return lax.ppermute(block, axis, route)]
  transfers between devices with their start and end apart: 3 -> 0, of which waited for: 2 -> 0; matrix products, arithmetic and copies ran while one was open for 22% -> 0% of each run, Pallas kernels for 0% -> 0%
where the time goes in v2:
time: 40.4 us; the launch traced here: 40.3 us
  Pallas kernels  38.6 us (96%)
  local copies, waits for them, and re-layouts  1.67 us (4%)
    pallas_call x1, Pallas kernels, local(): pl.pallas_call(functools.partial(kernel, n_z), out_shape=jax.ShapeDtypeSt...  38.6 us
    unnamed x1, local copies, waits for them, and re-layouts  1.67 us

profile of v2, /device:TPU:1, one launch (start us, length us, event | category | flops | bytes accessed | tf_op | source)
XLA Modules:
  0.0 40.3 jit_solution(8514444487947021778)
XLA Ops:
  0.0 38.6 %shard_map.127 = bf16[512,256]{1,0:T(8,128)(2,1)} custom-call(bf16[512,256]{1,0:T(8,128)(2,1)} %og_any.1, bf16[512,256]{1,0:T(8,128)(2,1)} %ig_any.1, bf16[512,256]{1,0:T(8,128)(2,1)} %vi_any.1, f32[128,256]{1,0:T(8,128)} %sf_any.1, f32[16,512]{1,0:T(8,128)} %bitcast.2, f32[1,256]{1,0:T(1,128)} %bitcast.3, bf16[128,192]{1,0:T(8,128)(2,1)} %constant.14.clone.colf_any, ...), custom_call_target="tpu_custom_call" | custom-call | tf_op jit(solution)/shard_map/pallas_call | solution.py:381
  38.6 1.7 %copy.15 = bf16[512,256]{1,0:T(8,128)(2,1)} copy(bf16[512,256]{1,0:T(8,128)(2,1)} %shard_map.127) | data formatting | bytes 524288

commit v3 on v2

--- a/solution.py
+++ b/solution.py
@@ -94,39 +94,15 @@
 def kernel(
     n_z,
     og_any, ig_any, vi_any, sf_any, lf_any, skip_any, colf_any, coli_any, rowf_any, rowi_any, turn_any, shf_any, shi_any,
-    out_any,
+    out,
     og, ig, vi, sf, lf, skip, colf, coli, rowf, rowi, turn, shf, shi,
     halo, vt, igt, skipt, taps, keep, fsend, frecv, msend, mrecv, tsend, trecv, rsend, rrecv, usend, urecv,
-    spec, xs, cross, carry, fin, outv,
-    in_sem, halo_sem, fs_sem, fr_sem, ms_sem, mr_sem, ts_sem, tr_sem, rs_sem, rr_sem, us_sem, ur_sem, out_sem,
+    spec, xs, cross, carry, fin,
+    in_sem, halo_sem, fs_sem, fr_sem, ms_sem, mr_sem, ts_sem, tr_sem, rs_sem, rr_sem, us_sem, ur_sem,
 ):
     n_dev = n_z * INNER
     half_z = n_z // 2
     half_dev = n_dev // 2
-    me = lax.axis_index("ctx")
-    my_z = me // INNER
-    my_in = me % INNER
-    my_core = me % 2
-    my_half = me // half_dev
-    tokens, chans = vi.shape
-    q_count = tokens // LANES
-    rows = half_dev * q_count
-    blocks = chans // LANES
-    per_block = LANES // OWN
-
-    inners = [(my_in + r) % INNER for r in range(INNER)]
-    turns = []
-    for d in range(1, n_z // 2):
-        turns += [d, -d]
-    turns += [n_z // 2, 0]
-    sign = 1 - 2 * my_core
-    planes = [((my_z + sign * d + n_z) % n_z) * INNER for d in turns]
-    peers = [z + i for z in planes for i in inners[1:] + inners[:1]][:-1]
-
-    barrier = pltpu.get_barrier_semaphore()
-    for p in peers:
-        pl.semaphore_signal(barrier, inc=1, device_id={"ctx": p}, device_id_type=MESH)
-
     order = [
         (vi_any, vi), (ig_any, ig), (shf_any, shf), (sf_any, sf), (lf_any, lf), (shi_any, shi), (og_any, og), (skip_any, skip),
         (colf_any, colf), (coli_any, coli), (rowf_any, rowf), (rowi_any, rowi), (turn_any, turn),
@@ -135,6 +111,37 @@
     for copy in loads:
         copy.start()
 
+    def wrap(x, n):
+        return jnp.where(x >= n, x - n, x)
+
+    me = lax.axis_index("ctx")
+    my_z = me // INNER
+    my_in = me - my_z * INNER
+    my_x = my_in // 2
+    my_core = my_in - my_x * 2
+    partner = me + 1 - 2 * my_core
+    my_half = jnp.where(my_z >= half_z, 1, 0)
+    tokens, chans = vi.shape
+    q_count = tokens // LANES
+    rows = half_dev * q_count
+    blocks = chans // LANES
+    parts = q_count // 2
+    per_block = LANES // OWN
+
+    inners = [my_in] + [wrap(my_in + r, INNER) for r in range(1, INNER)]
+    turns = []
+    for d in range(1, n_z // 2):
+        turns += [d, -d]
+    turns += [n_z // 2, 0]
+    ahead = {d: wrap(my_z + d + (n_z if d < 0 else 0), n_z) * INNER for d in turns}
+    flip = {d: (-d if -d in ahead else d) for d in turns}
+    planes = [jnp.where(my_core == 0, ahead[d], ahead[flip[d]]) for d in turns]
+    peers = [z + i for z in planes for i in inners[1:] + inners[:1]][:-1]
+
+    barrier = pltpu.get_barrier_semaphore()
+    for p in peers[: n_dev - INNER][::-1] + peers[n_dev - INNER :]:
+        pl.semaphore_signal(barrier, inc=1, device_id={"ctx": p}, device_id_type=MESH)
+
     def remote(src, dst, ssem, rsem, p):
         pltpu.make_async_remote_copy(
             src_ref=src, dst_ref=dst, send_sem=ssem, recv_sem=rsem, device_id={"ctx": p}, device_id_type=MESH
@@ -154,6 +161,16 @@
         vt[q + 1, lanes, :] = vi[toks, lanes].astype(F32).T.astype(BF16)
         igt[q, lanes, :] = ig[toks, lanes].astype(F32).T
 
+    last_in = (my_z >= n_z - n_z // 4) & (my_x == 1)
+
+    def enter():
+        pl.semaphore_wait(barrier, n_dev - 1)
+
+        @pl.when(me < n_dev - 1)
+        def _():
+            remote(vi_any.at[pl.ds(tokens - LANES, LANES), :], halo, halo_sem.at[0], halo_sem.at[1], me + 1)
+
+    pl.when(last_in)(enter)
     loads[0].wait()
     loads[1].wait()
     for q in range(q_count):
@@ -191,32 +208,41 @@
             wide = mm(high, shi[...])
             keep[q, lanes, :] = igt[q, lanes, :] * (wide[:, 0:LANES] + wide[:, LANES:] + mm(low, shi[:, 0:LANES]))
 
+    share = LANES // parts
+
     def pack(part):
         q = 2 * part
         top = peak(keep[q : q + 2].reshape(2 * chans, LANES))
-        tsend[part] = top
+        tsend[:, part * share : (part + 1) * share] = top[:, 0:share]
         first = encode(keep[q], top).reshape(n_dev, OWN, LANES)
         second = encode(keep[q + 1], top).reshape(n_dev, OWN, LANES)
         msend[part] = jnp.concatenate([first, second], axis=1).astype(BF16)
 
-    parts = q_count // 2
     for q in range(q_count - 1, 0, -1):
         short(q)
     for part in range(parts - 1, 0, -1):
         pack(part)
 
-    pl.semaphore_wait(barrier, n_dev - 1)
-    remote(vi.at[tokens - LANES :, :], halo, halo_sem.at[0], halo_sem.at[1], (me + 1) % n_dev)
-    send_all(lambda p: fsend.at[p // 2], frecv, fs_sem, fr_sem)
+    pl.when(jnp.logical_not(last_in))(enter)
 
     def send_part(part):
         send_all(lambda p: msend.at[part, p], mrecv.at[part], ms_sem.at[part], mr_sem.at[part, my_half])
-        send_all(lambda p: tsend.at[part], trecv.at[part], ts_sem.at[part], tr_sem.at[part, my_half])
-
+
+    my_pair = 2 * my_z + my_x
+    for k in range(n_dev // 2):
+        z, x = planes[k // 2], k % 2
+        g = (z // 2) + wrap(my_x + 1 - x, 2)
+        if k < n_dev // 2 - 1:
+            remote(fsend.at[g], frecv.at[my_core, my_pair], fs_sem.at[0], fr_sem.at[0], 2 * g + my_core)
+        else:
+            pltpu.make_async_copy(fsend.at[my_pair], frecv.at[my_core, my_pair], fr_sem.at[0]).start()
     for part in range(parts - 1, 0, -1):
         send_part(part)
 
-    pltpu.make_async_copy(halo, halo, halo_sem.at[1]).wait()
+    @pl.when(me > 0)
+    def _():
+        pltpu.make_async_copy(halo, halo, halo_sem.at[1]).wait()
+
     for b in range(blocks):
         lanes = slice(b * LANES, (b + 1) * LANES)
         before = halo[:, lanes].astype(F32).T
@@ -224,6 +250,9 @@
     short(0)
     pack(0)
     send_part(0)
+    send_all(lambda p: tsend, trecv, ts_sem, tr_sem.at[my_half])
+    arrived(frecv.at[my_core], fr_sem.at[0])
+    remote(frecv.at[my_core], frecv.at[my_core], fs_sem.at[1], fr_sem.at[1], partner)
 
     for i in range(6, len(order)):
         loads[i].wait()
@@ -265,10 +294,10 @@
             out.append(jnp.concatenate([re * h_re - im * h_im, re * h_im + im * h_re], axis=1))
         return jnp.concatenate(out, axis=0)
 
-    arrived(frecv, fr_sem)
+    arrived(frecv.at[0], fr_sem.at[1])
     for s in range(n_dev):
         which, at = s // half_dev, s % half_dev
-        fin[q_count * at : q_count * (at + 1), which * LANES : (which + 1) * LANES] = frecv[s]
+        fin[q_count * at : q_count * (at + 1), which * LANES : (which + 1) * LANES] = frecv[s % 2, s // 2]
     both = forward(fin[...]) * (1.0 / (rows * LANES))
     spec[0] = both[0:rows]
     spec[1] = both[rows:]
@@ -278,8 +307,17 @@
         got = []
         for part in range(parts):
             arrived(mrecv.at[part, span], mr_sem.at[part, half])
-            arrived(trecv.at[part, span], tr_sem.at[part, half])
-            got.append(decode(mrecv[part, span].astype(F32), trecv[part, span]))
+        arrived(trecv.at[span], tr_sem.at[half])
+        tops = trecv[span].reshape(half_dev, LANES)
+        for part in range(parts):
+            one = tops
+            if parts > 1:
+                at = lax.broadcasted_iota(jnp.int32, (half_dev, LANES), 1) // share
+                one = jnp.zeros_like(tops)
+                for k in range(parts):
+                    moved = pltpu.roll(tops, (k - part) * share % LANES, 1) if k != part else tops
+                    one = jnp.where(at == k, moved, one)
+            got.append(decode(mrecv[part, span].astype(F32), one.reshape(half_dev, 1, LANES)))
         xs[...] = jnp.concatenate(got, axis=1).reshape(rows * OWN, LANES)
         return jnp.concatenate([xs[pl.ds(c, rows, stride=OWN), :] for c in range(OWN)], axis=1)
 
@@ -292,7 +330,7 @@
             xs[pl.ds(c, rows, stride=OWN), :] = code[:, c * LANES : (c + 1) * LANES]
         rsend[half] = xs[...].reshape(half_dev, q_count * OWN, LANES).astype(BF16)
         for k in range(half_z):
-            z = (my_z + k) % half_z
+            z = wrap(wrap(my_z, half_z) + k, half_z) if k else wrap(my_z, half_z)
             for r in range(INNER):
                 at = z * INNER + inners[r]
                 p = half * half_dev + at
@@ -327,19 +365,21 @@
         total = decode(code, urecv[...]).reshape(chans, LANES) + skipt[...] * keep[q]
         for b in range(blocks):
             lanes = slice(b * LANES, (b + 1) * LANES)
-            outv[toks, lanes] = (og[toks, lanes].astype(F32) * total[lanes, :].T).astype(BF16)
-    done = pltpu.make_async_copy(outv, out_any, out_sem)
-    done.start()
+            out[toks, lanes] = (og[toks, lanes].astype(F32) * total[lanes, :].T).astype(BF16)
 
     sent = pl.ds(0, n_dev - 1)
-    arrived(halo, halo_sem.at[0])
-    arrived(frecv.at[sent], fs_sem)
+
+    @pl.when(me < n_dev - 1)
+    def _():
+        arrived(halo, halo_sem.at[0])
+
+    arrived(frecv.at[0, pl.ds(0, n_dev // 2 - 1)], fs_sem.at[0])
+    arrived(frecv.at[0], fs_sem.at[1])
     for part in range(parts):
         arrived(mrecv.at[part, sent], ms_sem.at[part])
-        arrived(trecv.at[part, sent], ts_sem.at[part])
+    arrived(trecv.at[sent], ts_sem)
     arrived(rrecv.at[sent], rs_sem)
     arrived(urecv.at[sent], us_sem)
-    done.wait()
 
 
 def local(n_z, output_gate, input_gate, value_input, short_filter, long_filter, skip_gain):
@@ -360,11 +400,11 @@
         pltpu.VMEM((3, chans, LANES), F32),
         pltpu.VMEM((q_count, chans, LANES), F32),
         pltpu.VMEM((n_dev // 2, q_count, LANES), F32),
-        pltpu.VMEM((n_dev, q_count, LANES), F32),
+        pltpu.VMEM((2, n_dev // 2, q_count, LANES), F32),
         pltpu.VMEM((parts, n_dev, 2 * OWN, LANES), BF16),
         pltpu.VMEM((parts, n_dev, 2 * OWN, LANES), BF16),
-        pltpu.VMEM((parts, 1, LANES), F32),
-        pltpu.VMEM((parts, n_dev, 1, LANES), F32),
+        pltpu.VMEM((1, LANES), F32),
+        pltpu.VMEM((n_dev, 1, LANES), F32),
         pltpu.VMEM((2, n_dev // 2, q_count * OWN, LANES), BF16),
         pltpu.VMEM((n_dev, q_count * OWN, LANES), BF16),
         pltpu.VMEM((2, 1, LANES), F32),
@@ -374,15 +414,14 @@
         pltpu.VMEM((rows * OWN, 2 * LANES), F32),
         pltpu.VMEM((rows, OWN * LANES), F32),
         pltpu.VMEM((rows, 2 * LANES), F32),
-        pltpu.VMEM((tokens, chans), BF16),
-        dma((len(operands),)), dma((2,)), dma, dma, dma((parts,)), dma((parts, 2)), dma((parts,)), dma((parts, 2)),
-        dma, dma, dma, dma, dma,
+        dma((len(operands),)), dma((2,)), dma((2,)), dma((2,)), dma((parts,)), dma((parts, 2)), dma, dma((2,)),
+        dma, dma, dma, dma,
     ]
     return pl.pallas_call(
         functools.partial(kernel, n_z),
-        out_shape=jax.ShapeDtypeStruct((tokens, chans), BF16),
+        out_shape=pltpu.VMEM((tokens, chans), BF16),
         in_specs=[pl.BlockSpec(memory_space=pl.ANY)] * len(operands),
-        out_specs=pl.BlockSpec(memory_space=pl.ANY),
+        out_specs=pl.BlockSpec(memory_space=pltpu.VMEM),
         scratch_shapes=scratch,
         compiler_params=pltpu.CompilerParams(collective_id=0, has_side_effects=True, vmem_limit_bytes=60 << 20),
     )(*operands)

time: 40.4 us -> 37.7 us (0.933)
  Pallas kernels: 38.6 us -> 36.8 us
  local copies, waits for them, and re-layouts: 1.67 us -> 0.71 us
    pallas_call x1, Pallas kernels: 38.6 us -> 36.8 us  [local(): pl.pallas_call(functools.partial(kernel, n_z), out_shape=pltpu.VMEM((toke...]
    unnamed x1, local copies, waits for them, and re-layouts: 1.67 us -> 0.71 us
where the time goes in v3:
time: 37.7 us; the launch traced here: 37.6 us
  Pallas kernels  36.8 us (98%)
  local copies, waits for them, and re-layouts  0.71 us (2%)
    pallas_call x1, Pallas kernels, local(): pl.pallas_call(functools.partial(kernel, n_z), out_shape=pltpu.VMEM((toke...  36.8 us

profile of v3, /device:TPU:1, one launch (start us, length us, event | category | flops | bytes accessed | tf_op | source)
XLA Modules:
  0.0 37.6 jit_solution(9497702997923698479)
XLA Ops:
  0.0 36.8 %shard_map.127 = bf16[512,256]{1,0:T(8,128)(2,1)S(1)} custom-call(bf16[512,256]{1,0:T(8,128)(2,1)} %og_any.1, bf16[512,256]{1,0:T(8,128)(2,1)} %ig_any.1, bf16[512,256]{1,0:T(8,128)(2,1)} %vi_any.1, f32[128,256]{1,0:T(8,128)} %sf_any.1, f32[16,512]{1,0:T(8,128)} %bitcast.2, f32[1,256]{1,0:T(1,128)} %bitcast.3, bf16[128,192]{1,0:T(8,128)(2,1)} %constant.14.clone.colf_any, ...), custom_call_target="tpu_custom_call" | custom-call | tf_op jit(solution)/shard_map/pallas_call | solution.py:420
  36.9 0.7 %copy.15 = bf16[512,256]{1,0:T(8,128)(2,1)} copy(bf16[512,256]{1,0:T(8,128)(2,1)S(1)} %shard_map.127) | data formatting | bytes 524288

commit v4 on v3

--- a/solution.py
+++ b/solution.py
@@ -97,7 +97,7 @@
     out,
     og, ig, vi, sf, lf, skip, colf, coli, rowf, rowi, turn, shf, shi,
     halo, vt, igt, skipt, taps, keep, fsend, frecv, msend, mrecv, tsend, trecv, rsend, rrecv, usend, urecv,
-    spec, xs, cross, carry, fin,
+    spec, xs, cross, carry, ready, fin,
     in_sem, halo_sem, fs_sem, fr_sem, ms_sem, mr_sem, ts_sem, tr_sem, rs_sem, rr_sem, us_sem, ur_sem,
 ):
     n_dev = n_z * INNER
@@ -129,17 +129,17 @@
     per_block = LANES // OWN
 
     inners = [my_in] + [wrap(my_in + r, INNER) for r in range(1, INNER)]
-    turns = []
-    for d in range(1, n_z // 2):
+    turns = [n_z // 2]
+    for d in range(n_z // 2 - 1, 0, -1):
         turns += [d, -d]
-    turns += [n_z // 2, 0]
+    turns += [0]
     ahead = {d: wrap(my_z + d + (n_z if d < 0 else 0), n_z) * INNER for d in turns}
     flip = {d: (-d if -d in ahead else d) for d in turns}
     planes = [jnp.where(my_core == 0, ahead[d], ahead[flip[d]]) for d in turns]
     peers = [z + i for z in planes for i in inners[1:] + inners[:1]][:-1]
 
     barrier = pltpu.get_barrier_semaphore()
-    for p in peers[: n_dev - INNER][::-1] + peers[n_dev - INNER :]:
+    for p in peers:
         pl.semaphore_signal(barrier, inc=1, device_id={"ctx": p}, device_id_type=MESH)
 
     def remote(src, dst, ssem, rsem, p):
@@ -249,8 +249,8 @@
         vt[0, lanes, :] = jnp.where(me > 0, before, 0.0).astype(BF16)
     short(0)
     pack(0)
+    send_all(lambda p: tsend, trecv, ts_sem, tr_sem.at[my_half])
     send_part(0)
-    send_all(lambda p: tsend, trecv, ts_sem, tr_sem.at[my_half])
     arrived(frecv.at[my_core], fr_sem.at[0])
     remote(frecv.at[my_core], frecv.at[my_core], fs_sem.at[1], fr_sem.at[1], partner)
 
@@ -273,7 +273,7 @@
             pieces.append(jnp.concatenate([re * turn_re - im * turn_im, re * turn_im + im * turn_re], axis=1))
         return along(jnp.concatenate(pieces, axis=0), rowf[...])
 
-    def backward(block, keep_rows):
+    def backward(block):
         mid = along(block, rowi[...])
         reals, imags = [], []
         for c in range(OWN):
@@ -282,7 +282,7 @@
             reals.append(re * turn_re + im * turn_im)
             imags.append(im * turn_re - re * turn_im)
         high, low = halves(jnp.concatenate([jnp.concatenate(reals, axis=1), jnp.concatenate(imags, axis=1)], axis=0))
-        return mm(coli[0:keep_rows, :], jnp.concatenate([high, low, high], axis=0))
+        return jnp.concatenate([high, low, high], axis=0)
 
     def times(spectra, which):
         h_re = spec[which, :, 0:LANES]
@@ -329,33 +329,32 @@
         for c in range(OWN):
             xs[pl.ds(c, rows, stride=OWN), :] = code[:, c * LANES : (c + 1) * LANES]
         rsend[half] = xs[...].reshape(half_dev, q_count * OWN, LANES).astype(BF16)
-        for k in range(half_z):
-            z = wrap(wrap(my_z, half_z) + k, half_z) if k else wrap(my_z, half_z)
-            for r in range(INNER):
-                at = z * INNER + inners[r]
+        for z in range(half_z):
+            for i in inners[1:] + inners[:1]:
+                at = z * INNER + i
                 p = half * half_dev + at
 
                 def away():
                     remote(rsend.at[half, at], rrecv.at[me], rs_sem, rr_sem, p)
                     remote(usend.at[half], urecv.at[me], us_sem, ur_sem, p)
 
-                if k or r:
+                if i is not inners[0]:
                     away()
-                else:
-                    pl.when(my_half != half)(away)
-
-                    @pl.when(my_half == half)
-                    def _():
-                        pltpu.make_async_copy(rsend.at[half, at], rrecv.at[me], rr_sem).start()
-                        pltpu.make_async_copy(usend.at[half], urecv.at[me], ur_sem).start()
+                    continue
+                pl.when(my_z != half * half_z + z)(away)
+
+                @pl.when(my_z == half * half_z + z)
+                def _():
+                    pltpu.make_async_copy(rsend.at[half, at], rrecv.at[me], rr_sem).start()
+                    pltpu.make_async_copy(usend.at[half], urecv.at[me], ur_sem).start()
 
     spectra = forward(owned(0))
-    result = backward(times(spectra, 0), 2 * rows)
-    carry[...] = result[rows:]
-    give_back(0, result[0:rows])
+    ready[...] = backward(times(spectra, 0))
+    give_back(0, mm(coli[0:rows, :], ready[...]))
+    carry[...] = mm(coli[rows:, :], ready[...])
     cross[...] = times(spectra, 1)
     spectra = forward(owned(1))
-    give_back(1, backward(times(spectra, 0) + cross[...], rows) + carry[...])
+    give_back(1, mm(coli[0:rows, :], backward(times(spectra, 0) + cross[...])) + carry[...])
 
     arrived(rrecv, rr_sem)
     arrived(urecv, ur_sem)
@@ -413,6 +412,7 @@
         pltpu.VMEM((rows * OWN, LANES), F32),
         pltpu.VMEM((rows * OWN, 2 * LANES), F32),
         pltpu.VMEM((rows, OWN * LANES), F32),
+        pltpu.VMEM((6 * rows, OWN * LANES), BF16),
         pltpu.VMEM((rows, 2 * LANES), F32),
         dma((len(operands),)), dma((2,)), dma((2,)), dma((2,)), dma((parts,)), dma((parts, 2)), dma, dma((2,)),
         dma, dma, dma, dma,

time: 37.7 us -> 36.5 us (0.968)
  Pallas kernels: 36.8 us -> 35.7 us
    pallas_call x1, Pallas kernels: 36.8 us -> 35.7 us  [local(): pl.pallas_call(functools.partial(kernel, n_z), out_shape=pltpu.VMEM((toke...]
where the time goes in v4:
time: 36.5 us; the launch traced here: 36.4 us
  Pallas kernels  35.7 us (98%)
  local copies, waits for them, and re-layouts  0.71 us (2%)
    pallas_call x1, Pallas kernels, local(): pl.pallas_call(functools.partial(kernel, n_z), out_shape=pltpu.VMEM((toke...  35.7 us

profile of v4, /device:TPU:1, one launch (start us, length us, event | category | flops | bytes accessed | tf_op | source)
XLA Modules:
  0.0 36.4 jit_solution(7355377892583937061)
XLA Ops:
  0.0 35.7 %shard_map.127 = bf16[512,256]{1,0:T(8,128)(2,1)S(1)} custom-call(bf16[512,256]{1,0:T(8,128)(2,1)} %og_any.1, bf16[512,256]{1,0:T(8,128)(2,1)} %ig_any.1, bf16[512,256]{1,0:T(8,128)(2,1)} %vi_any.1, f32[128,256]{1,0:T(8,128)} %sf_any.1, f32[16,512]{1,0:T(8,128)} %bitcast.2, f32[1,256]{1,0:T(1,128)} %bitcast.3, bf16[128,192]{1,0:T(8,128)(2,1)} %constant.14.clone.colf_any, ...), custom_call_target="tpu_custom_call" | custom-call | tf_op jit(solution)/shard_map/pallas_call | solution.py:420
  35.7 0.7 %copy.15 = bf16[512,256]{1,0:T(8,128)(2,1)} copy(bf16[512,256]{1,0:T(8,128)(2,1)S(1)} %shard_map.127) | data formatting | bytes 524288

commit v5 on v4

--- a/solution.py
+++ b/solution.py
@@ -41,8 +41,10 @@
     col_inv = np.concatenate([hi, hi, lo], 1)
     cos2, sin2 = np.cos(second), np.sin(second)
     row = np.block([[cos2, sin2], [-sin2, cos2]])
-    row_fwd = np.concatenate(split_np(row), 0)
-    row_inv = np.concatenate(split_np(row.T), 0)
+    hi, lo = split_np(row)
+    row_fwd = np.concatenate([hi, hi, lo], 0)
+    hi, lo = split_np(row.T)
+    row_inv = np.concatenate([hi, hi, lo], 0)
     turn = np.concatenate([np.cos(twist), np.sin(twist)], 0).astype(np.float32)
     return col_fwd, col_inv, row_fwd, row_inv, turn
 
@@ -87,8 +89,7 @@
 
 def along(block, table):
     high, low = halves(block)
-    main = table[0 : 2 * LANES, :]
-    return mm(high, main) + mm(low, main) + mm(high, table[2 * LANES :, :])
+    return mm(jnp.concatenate([high, low, high], axis=1), table)
 
 
 def kernel(
@@ -200,7 +201,7 @@
         for b in range(blocks):
             lanes = slice(b * LANES, (b + 1) * LANES)
             window = jnp.concatenate([vt[q, lanes, :], vt[q + 1, lanes, :]], axis=1)
-            freq = mm(window, shf[0 : 2 * LANES, :]) + mm(window, shf[2 * LANES :, :])
+            freq = mm(jnp.concatenate([window, window], axis=1), shf[...])
             re, im = freq[:, 0:LANES], freq[:, LANES:]
             f_re, f_zero, f_top = taps[0, lanes, :], taps[1, lanes, :], taps[2, lanes, :]
             prod = jnp.concatenate([re * f_re - im * f_zero, re * f_zero + im * f_top], axis=1)

time: 36.5 us -> 36.5 us (level)
  no operation moved by 1% of the time
where the time goes in v5:
time: 36.5 us; the launch traced here: 36.4 us
  Pallas kernels  35.6 us (98%)
  local copies, waits for them, and re-layouts  0.71 us (2%)
    pallas_call x1, Pallas kernels, local(): pl.pallas_call(functools.partial(kernel, n_z), out_shape=pltpu.VMEM((toke...  35.6 us

profile of v5, /device:TPU:1, one launch (start us, length us, event | category | flops | bytes accessed | tf_op | source)
XLA Modules:
  0.0 36.4 jit_solution(47781372554992576)
XLA Ops:
  0.0 35.6 %shard_map.127 = bf16[512,256]{1,0:T(8,128)(2,1)S(1)} custom-call(bf16[512,256]{1,0:T(8,128)(2,1)} %og_any.1, bf16[512,256]{1,0:T(8,128)(2,1)} %ig_any.1, bf16[512,256]{1,0:T(8,128)(2,1)} %vi_any.1, f32[128,256]{1,0:T(8,128)} %sf_any.1, f32[16,512]{1,0:T(8,128)} %bitcast.2, f32[1,256]{1,0:T(1,128)} %bitcast.3, bf16[128,192]{1,0:T(8,128)(2,1)} %constant.14.clone.colf_any, ...), custom_call_target="tpu_custom_call" | custom-call | tf_op jit(solution)/shard_map/pallas_call | solution.py:421
  35.6 0.7 %copy.15 = bf16[512,256]{1,0:T(8,128)(2,1)} copy(bf16[512,256]{1,0:T(8,128)(2,1)S(1)} %shard_map.127) | data formatting | bytes 524288

commit v6 on v5

--- a/solution.py
+++ b/solution.py
@@ -357,12 +357,14 @@
     spectra = forward(owned(1))
     give_back(1, mm(coli[0:rows, :], backward(times(spectra, 0) + cross[...])) + carry[...])
 
+    for q in range(q_count):
+        keep[q] = skipt[...] * keep[q]
     arrived(rrecv, rr_sem)
     arrived(urecv, ur_sem)
     for q in range(q_count):
         toks = slice(q * LANES, (q + 1) * LANES)
         code = rrecv[:, (q // 2) * 2 * OWN : (q // 2 + 1) * 2 * OWN, :].astype(F32)[:, (q % 2) * OWN : (q % 2 + 1) * OWN, :]
-        total = decode(code, urecv[...]).reshape(chans, LANES) + skipt[...] * keep[q]
+        total = decode(code, urecv[...]).reshape(chans, LANES) + keep[q]
         for b in range(blocks):
             lanes = slice(b * LANES, (b + 1) * LANES)
             out[toks, lanes] = (og[toks, lanes].astype(F32) * total[lanes, :].T).astype(BF16)

time: 36.5 us -> 36.5 us (level)
  no operation moved by 1% of the time
where the time goes in v6:
time: 36.5 us; the launch traced here: 36.3 us
  Pallas kernels  35.6 us (98%)
  local copies, waits for them, and re-layouts  0.71 us (2%)
    pallas_call x1, Pallas kernels, local(): pl.pallas_call(functools.partial(kernel, n_z), out_shape=pltpu.VMEM((toke...  35.6 us

profile of v6, /device:TPU:1, one launch (start us, length us, event | category | flops | bytes accessed | tf_op | source)
XLA Modules:
  0.0 36.3 jit_solution(4406002175427996619)
XLA Ops:
  0.0 35.6 %shard_map.127 = bf16[512,256]{1,0:T(8,128)(2,1)S(1)} custom-call(bf16[512,256]{1,0:T(8,128)(2,1)} %og_any.1, bf16[512,256]{1,0:T(8,128)(2,1)} %ig_any.1, bf16[512,256]{1,0:T(8,128)(2,1)} %vi_any.1, f32[128,256]{1,0:T(8,128)} %sf_any.1, f32[16,512]{1,0:T(8,128)} %bitcast.2, f32[1,256]{1,0:T(1,128)} %bitcast.3, bf16[128,192]{1,0:T(8,128)(2,1)} %constant.14.clone.colf_any, ...), custom_call_target="tpu_custom_call" | custom-call | tf_op jit(solution)/shard_map/pallas_call | solution.py:423
  35.6 0.7 %copy.15 = bf16[512,256]{1,0:T(8,128)(2,1)} copy(bf16[512,256]{1,0:T(8,128)(2,1)S(1)} %shard_map.127) | data formatting | bytes 524288
